TPU v7x, 128 devices: a whole 4x4x4 slice. The times are simulated.
128 devices in a mesh: bricks: 128 (over y, z, x, core).
Axes of the slice: x: 4, y: 4, z: 4, core: 2. Of those that a mesh axis runs over, the one named last changes fastest.
Arguments:
- calcium: float32 [256, 32, 1024], P('bricks'), may hold values from 0.2 to 1.5
- buffer: float32 [256, 32, 1024], P('bricks'), may hold values from 0.1 to 1.5
- fraction: float32 [256, 32, 1024], P('bricks'), may hold values from 0.1 to 0.4
- rates: float32 [256, 3, 2], P('bricks'), may hold values from 2 to 64
- inverses: float32 [256, 3, 2, 32, 32], P('bricks'), as said below
- neighbors: int32 [3, 2, 256], replicated, may hold values from -1 to 255, as said below
- ranks: int32 [3, 256], replicated, may hold values from 0 to 31, as said below
Outputs:
- calcium_next: float32 [256, 32, 1024], P('bricks')
- buffer_next: float32 [256, 32, 1024], P('bricks')
Inputs may be any that keep to these rules, and one draw needn't show every extreme that they name: neighbors[d, 0, s] and neighbors[d, 1, s] are the slots of the active bricks adjacent to slot s before and after it along dimension d of a block of 32 x 16 x 2 brick positions, -1 where that position is inactive or outside; active bricks fill whole rows along the first dimension. ranks[d, s] is the number of consecutive active bricks before slot s along dimension d. inverses[s, d, k] is the inverse of I + rates[s, d, k] K, K the 32 x 32 second difference with diagonal 1, 2, ..., 2, 1 and off-diagonals -1.
All inputs are finite; a program needn't handle non-finite values.
Results may differ from a plain program's by a relative error of at most 0.00015.
Values sent between devices are 32-bit elements; how exact they have to be, the bound alone decides.
A program may use at most 128 MiB of HBM per device.

v0:
```python
from functools import partial

import jax
import jax.numpy as jnp
from jax import lax
from jax.sharding import PartitionSpec as P

GX = 32


KON = 0.5
KOFF = 0.3
BTOT = 2.0
INFLUX = 0.1


def fetch(table, index):
    rows = jnp.take(table, jnp.maximum(index, 0), axis=0)
    has = (index >= 0).reshape((-1,) + (1,) * (rows.ndim - 1))
    return jnp.where(has, rows, jnp.zeros_like(rows))


def lookup(planes, before, after):
    sides = []
    for d in range(3):
        lower = fetch(planes[:, d, 1], before[d])
        upper = fetch(planes[:, d, 0], after[d])
        sides.append(jnp.stack([lower, upper], 1))
    return jnp.stack(sides, 1)


def coupling(rate_all, neighbors):
    per_dim = []
    for d in range(3):
        mine = rate_all[:, d]
        sides = []
        for side in range(2):
            other = fetch(mine, neighbors[d, side])
            has = (neighbors[d, side] >= 0)[:, None]
            sides.append(jnp.where(has, 2.0 * mine * other / (mine + other), jnp.zeros_like(mine)))
        per_dim.append(jnp.stack(sides, 1))
    return jnp.stack(per_dim, 1)


def end_planes(field):
    count, edge = (field.shape[0], field.shape[2])
    per_dim = []
    for d in range(3):
        first = lax.index_in_dim(field, 0, 2 + d, False).reshape(count, 2, edge * edge)
        last = lax.index_in_dim(field, edge - 1, 2 + d, False).reshape(count, 2, edge * edge)
        per_dim.append(jnp.stack([first, last], 1))
    return jnp.stack(per_dim, 1)


def operator(field, d, rate, glow, gup, hlow, hup):
    axis = 2 + d
    edge = field.shape[axis]
    plane_shape = lax.index_in_dim(field, 0, axis, False).shape
    lower_face = jnp.expand_dims(hlow.reshape(plane_shape), axis)
    upper_face = jnp.expand_dims(hup.reshape(plane_shape), axis)
    upper = jnp.concatenate([lax.slice_in_dim(field, 1, edge, axis=axis), upper_face], axis)
    lower = jnp.concatenate([lower_face, lax.slice_in_dim(field, 0, edge - 1, axis=axis)], axis)
    place = lax.broadcasted_iota(jnp.int32, field.shape, axis)
    inner = rate[:, :, None, None, None]
    c_up = jnp.where(place == edge - 1, gup[:, :, None, None, None], inner)
    c_down = jnp.where(place == 0, glow[:, :, None, None, None], inner)
    return c_up * (upper - field) + c_down * (lower - field)


def reaction(field, fraction):
    count, edge = (field.shape[0], field.shape[2])
    alpha = fraction.reshape(count, edge, edge, edge)
    calc, bound = (field[:, 0], field[:, 1])
    bind = KON * calc * (BTOT - bound) - KOFF * bound
    return jnp.stack([-bind + INFLUX * (1.0 - alpha) / alpha, bind], 1)


def apply_inverse(block, field, d):
    forms = ["psab,psbjk->psajk", "psab,psibk->psiak", "psab,psijb->psija"]
    return jnp.einsum(forms[d], block, field, precision=lax.Precision.HIGHEST)


def line_ends(field, d):
    count, edge = (field.shape[0], field.shape[2])
    first = lax.index_in_dim(field, 0, 2 + d, False).reshape(count, 2, edge * edge)
    last = lax.index_in_dim(field, edge - 1, 2 + d, False).reshape(count, 2, edge * edge)
    return jnp.stack([first, last], 2)


def block_terms(glow, gup, corner):
    v_first, v_last, w_first, w_last = (
        corner[..., 0],
        corner[..., 1],
        corner[..., 2],
        corner[..., 3],
    )
    a00 = 1.0 + glow * v_first
    a01 = gup * w_first
    a10 = glow * v_last
    a11 = 1.0 + gup * w_last
    lq0 = -glow * v_first
    lq1 = -glow * v_last
    up0 = -gup * w_first
    up1 = -gup * w_last
    return (a00, a01, a10, a11, lq0, lq1, up0, up1)


def chain_order(before, rank):
    slots = jnp.arange(before.shape[0], dtype=jnp.int32)
    pointer = jnp.where(before >= 0, before, slots)
    for step in range(GX.bit_length()):
        pointer = jnp.take(pointer, pointer, axis=0)
    sort_key = pointer * GX + rank
    order = jnp.argsort(sort_key)
    inverse_order = jnp.argsort(order)
    return (order, inverse_order)


def shift_down(values):
    return jnp.concatenate([jnp.zeros_like(values[:1]), values[:-1]], 0)


def shift_up(values):
    return jnp.concatenate([values[1:], jnp.zeros_like(values[:1])], 0)


def compose_maps(first_map, second_map):
    e00, e01, e10, e11 = first_map
    l00, l01, l10, l11 = second_map
    n00 = l00 * e00 + l01 * e10
    n01 = l00 * e01 + l01 * e11
    n10 = l10 * e00 + l11 * e10
    n11 = l10 * e01 + l11 * e11
    scale = jnp.abs(n00) + jnp.abs(n01) + jnp.abs(n10) + jnp.abs(n11)
    return (n00 / scale, n01 / scale, n10 / scale, n11 / scale)


def compose_affine(first_map, second_map):
    first_q, first_p = first_map
    second_q, second_p = second_map
    return (first_q * second_q, second_p + second_q * first_p)


def sorted_solve(glow, gup, corner, before, after, order, inverse_order, ends):
    glow = jnp.take(glow, order, axis=0)
    gup = jnp.take(gup, order, axis=0)
    corner = jnp.take(corner, order, axis=0)
    has_b = jnp.take(before, order, axis=0) >= 0
    has_a = jnp.take(after, order, axis=0) >= 0
    arranged = jnp.take(ends, order, axis=0)
    y0 = arranged[:, :, 0]
    y1 = arranged[:, :, 1]
    a00, a01, a10, a11, lq0, lq1, up0, up1 = block_terms(glow, gup, corner)
    maps = (
        -(lq0 * up1 - lq1 * up0),
        a00 * up1 - a10 * up0,
        -(lq0 * a11 - a01 * lq1),
        a00 * a11 - a01 * a10,
    )
    summed = lax.associative_scan(compose_maps, maps, axis=0)
    f1_prev = summed[1] / summed[3]
    fq = shift_down(f1_prev)
    b00 = a00 - lq0 * fq
    b10 = a10 - lq1 * fq
    det = b00 * a11 - a01 * b10
    f0 = (a11 * up0 - a01 * up1) / det
    f1 = (b00 * up1 - b10 * up0) / det
    slope = (-(b00 * lq1 - b10 * lq0) / det)[:, :, None]
    offset = (b00[:, :, None] * y1 - b10[:, :, None] * y0) / det[:, :, None]
    e1 = lax.associative_scan(compose_affine, (slope, offset), axis=0)[1]
    eq = shift_down(e1)
    e0 = (
        a11[:, :, None] * y0 - a01[:, :, None] * y1 - (a11 * lq0 - a01 * lq1)[:, :, None] * eq
    ) / det[:, :, None]
    zp = lax.associative_scan(compose_affine, (-f0[:, :, None], e0), reverse=True, axis=0)[1]
    pn = shift_up(zp)
    zq = e1 - f1[:, :, None] * pn
    low = jnp.where(has_b[:, None, None], zp - shift_down(zq), jnp.zeros_like(zp))
    high = jnp.where(has_a[:, None, None], zq - pn, jnp.zeros_like(zq))
    return jnp.take(jnp.stack([low, high], 2), inverse_order, axis=0)


def correct(local, block, glow, gup, jumps, d):
    axis = 2 + d
    count, edge = (local.shape[0], local.shape[2])
    shape_v = [count, 2, 1, 1, 1]
    shape_v[axis] = edge
    first_col = block[..., 0].reshape(shape_v)
    last_col = block[..., edge - 1].reshape(shape_v)
    plane_shape = lax.index_in_dim(local, 0, axis, False).shape
    low = jnp.expand_dims(jumps[:, :, 0].reshape(plane_shape), axis)
    high = jnp.expand_dims(jumps[:, :, 1].reshape(plane_shape), axis)
    return (
        local
        - glow[:, :, None, None, None] * low * first_col
        - gup[:, :, None, None, None] * high * last_col
    )


def body(calcium, buffer, fraction, rates, inverses, neighbors, ranks):
    count, edge = (calcium.shape[0], calcium.shape[1])
    devices = lax.axis_size("bricks")
    square = edge * edge
    per_device = square // devices
    start = lax.axis_index("bricks") * count
    corners = jnp.stack(
        [
            inverses[..., 0, 0],
            inverses[..., edge - 1, 0],
            inverses[..., 0, edge - 1],
            inverses[..., edge - 1, edge - 1],
        ],
        -1,
    )
    rate_all, corner_all = (
        lax.all_gather(rates, "bricks", axis=0, tiled=True),
        lax.all_gather(corners, "bricks", axis=0, tiled=True),
    )
    couple_all = coupling(rate_all, neighbors)
    couple = lax.dynamic_slice_in_dim(couple_all, start, count, 0)
    field = jnp.stack([calcium, buffer], 1).reshape(count, 2, edge, edge, edge)
    planes = end_planes(field).reshape(count, 3, 2, 2, devices, per_device)
    lined = lookup(
        lax.all_to_all(planes, "bricks", split_axis=4, concat_axis=0, tiled=True),
        neighbors[:, 0],
        neighbors[:, 1],
    )
    halos = lax.all_to_all(lined, "bricks", split_axis=0, concat_axis=4, tiled=True).reshape(
        count, 3, 2, 2, square
    )
    lams = [
        operator(
            field, d, rates[:, d], couple[:, d, 0], couple[:, d, 1], halos[:, d, 0], halos[:, d, 1]
        )
        for d in range(3)
    ]
    rhs = field + lams[0] + 2.0 * lams[1] + 2.0 * lams[2] + reaction(field, fraction)

    def solve(right, d):
        block = inverses[:, d]
        local = apply_inverse(block, right, d)
        ends = line_ends(local, d).reshape(count, 2, 2, devices, per_device)
        order, inverse_order = chain_order(neighbors[d, 0], ranks[d])
        chain_fn = partial(
            sorted_solve,
            couple_all[:, d, 0],
            couple_all[:, d, 1],
            corner_all[:, d],
            neighbors[d, 0],
            neighbors[d, 1],
            order,
            inverse_order,
        )
        lined_jumps = chain_fn(
            lax.all_to_all(ends, "bricks", split_axis=3, concat_axis=0, tiled=True)[:, :, :, 0]
        )[:, :, :, None]
        jumps = lax.all_to_all(
            lined_jumps, "bricks", split_axis=0, concat_axis=3, tiled=True
        ).reshape(count, 2, 2, square)
        return correct(local, block, couple[:, d, 0], couple[:, d, 1], jumps, d)

    first = solve(rhs, 0)
    second = solve(first - lams[1], 1)
    third = solve(second - lams[2], 2)
    result = third.reshape(count, 2, edge, edge * edge)
    return (result[:, 0], result[:, 1])


def solution(mesh):
    in_specs = (
        P("bricks", None, None),
        P("bricks", None, None),
        P("bricks", None, None),
        P("bricks", None, None),
        P("bricks", None, None, None, None),
        P(),
        P(),
    )
    out_specs = (P("bricks", None, None), P("bricks", None, None))
    return jax.shard_map(body, mesh=mesh, in_specs=in_specs, out_specs=out_specs, check_vma=False)
```

profile of v0, /device:TPU:1, one launch (start us, length us, event | category | flops | bytes accessed | tf_op | source)
XLA Modules:
  0.0 658.5 jit_solution(8018914261589705422)
XLA Ops:
  5.6 5.8 divide_add_fusion
  23.9 4.2 reshape.1049
  28.1 12.3 %all-to-all-start = ((f32[128,1,192]{2,1,0:T(1,128)}), f32[128,1,192]{2,1,0:T(1,128)}, u32[]{:S(2)}, u32[]{:S(2)}) async-start(f32[128,1,192]{2,1,0:T(1,128)} %reshape.1049), calls=%async_computation | async-start | bytes 262144 | tf_op jit(solution)/shard_map/all_to_all | solution.py:224
  63.8 38.2 %all_gather.7 = f32[256,3,2,4]{1,2,0,3:T(2,128)S(1)} all-gather(f32[2,3,2,4]{1,2,0,3:T(2,128)S(1)} %pad_maximum_fusion.7), channel_id=1, replica_groups=mesh['bricks'=128] {'bricks'}, dimensions={0}, use_global_device_ids=true | all-gather | bytes 24768 | tf_op jit(solution)/shard_map/all_gather | solution.py:217
  102.1 3.6 fusion.208
  114.2 33.5 %all_gather.6 = f32[256,3,2]{1,2,0:T(2,128)S(1)} all-gather(f32[2,3,2]{1,2,0:T(2,128)S(1)} %copy-done.20), channel_id=1, replica_groups=mesh['bricks'=128] {'bricks'}, dimensions={0}, use_global_device_ids=true | all-gather | bytes 6192 | tf_op jit(solution)/shard_map/all_gather | solution.py:216
  374.5 4.2 reshape.1051
  378.8 5.8 all-to-all-start.1
  384.6 9.9 %all-to-all-done.1 = f32[128,1,192]{2,1,0:T(1,128)S(1)} async-done(((f32[128,1,192]{2,1,0:T(1,128)}), f32[128,1,192]{2,1,0:T(1,128)S(1)}, u32[]{:S(2)}, u32[]{:S(2)}) %all-to-all-start.1) | async-done | bytes 98336 | tf_op jit(solution)/shard_map/all_to_all | solution.py:228
  410.5 4.8 fusion.18
  417.5 3.8 fusion.31
  424.3 4.2 all-to-all-start.2
  477.1 9.7 %all-to-all-start.3 = ((f32[256,2,2,1,8]{4,2,1,3,0:T(2,128)}), f32[256,2,2,1,8]{4,2,1,3,0:T(2,128)S(1)}, u32[]{:S(2)}, u32[]{:S(2)}) async-start(f32[256,2,2,1,8]{4,2,1,3,0:T(2,128)} %select_bitcast_fusion.2), calls=%async_computation.3 | async-start | bytes 1048576 | tf_op jit(solution)/shard_map/all_to_all | solution.py:257
  487.7 12.5 %all-to-all-done.3 = f32[256,2,2,1,8]{4,2,1,3,0:T(2,128)S(1)} async-done(((f32[256,2,2,1,8]{4,2,1,3,0:T(2,128)}), f32[256,2,2,1,8]{4,2,1,3,0:T(2,128)S(1)}, u32[]{:S(2)}, u32[]{:S(2)}) %all-to-all-start.3) | async-done | bytes 32800 | tf_op jit(solution)/shard_map/all_to_all | solution.py:257
  501.1 3.7 subtract_subtract_fusion.1
  504.9 3.2 fusion.25
  511.0 4.9 all-to-all-start.4
  556.6 9.6 %all-to-all-start.5 = ((f32[256,2,2,1,8]{4,1,2,3,0:T(2,128)}), f32[256,2,2,1,8]{4,1,2,3,0:T(2,128)S(1)}, u32[]{:S(2)}, u32[]{:S(2)}) async-start(f32[256,2,2,1,8]{4,1,2,3,0:T(2,128)} %copy.2505), calls=%async_computation.5 | async-start | bytes 1048576 | tf_op jit(solution)/shard_map/all_to_all | solution.py:257
  566.6 13.1 %all-to-all-done.5 = f32[256,2,2,1,8]{4,1,2,3,0:T(2,128)S(1)} async-done(((f32[256,2,2,1,8]{4,1,2,3,0:T(2,128)}), f32[256,2,2,1,8]{4,1,2,3,0:T(2,128)S(1)}, u32[]{:S(2)}, u32[]{:S(2)}) %all-to-all-start.5) | async-done | bytes 32800 | tf_op jit(solution)/shard_map/all_to_all | solution.py:257
  580.5 3.7 subtract_subtract_fusion
  584.3 9.1 %fusion.23 = f32[2,2,32,32,32]{3,4,2,1,0:T(8,128)S(1)} fusion(f32[2,2,32,32,32]{4,2,3,1,0:T(8,128)S(1)} %subtract_subtract_fusion, f32[2,3,2,32,32]{4,3,2,1,0:T(8,128)S(1)} %copy-done.18), kind=kOutput, calls=%fused_computation.78 | convolution fusion | flops 50331648 | bytes 2686976 | tf_op jit(solution)/shard_map/psab,psijb->psija/dot_general | solution.py:80
  595.3 4.9 all-to-all-start.6
  602.2 11.5 %all-to-all-done.6 = f32[2,2,2,128,8]{4,1,0,2,3:T(2,128)S(1)} async-done(((f32[2,2,2,128,8]{4,1,0,2,3:T(2,128)}), f32[2,2,2,128,8]{4,1,0,2,3:T(2,128)S(1)}, u32[]{:S(2)}, u32[]{:S(2)}) %all-to-all-start.6) | async-done | bytes 32800 | tf_op jit(solution)/shard_map/all_to_all | solution.py:255
  633.6 18.0 %all_to_all.123 = f32[256,2,2,1,8]{4,1,2,3,0:T(2,128)S(1)} all-to-all(f32[256,2,2,1,8]{4,1,2,3,0:T(2,128)S(1)} %copy.2524), channel_id=1, replica_groups=mesh['bricks'=128] {'bricks'}, dimensions={0} | all-to-all | bytes 65536 | tf_op jit(solution)/shard_map/all_to_all | solution.py:257
  (2122 shorter events, 416.2 us)
Async XLA Ops:
  28.1 308.1 %all-to-all-start = ((f32[128,1,192]{2,1,0:T(1,128)}), f32[128,1,192]{2,1,0:T(1,128)}, u32[]{:S(2)}, u32[]{:S(2)}) async-start(f32[128,1,192]{2,1,0:T(1,128)} %reshape.1049), calls=%async_computation | async-start | bytes 262144 | tf_op jit(solution)/shard_map/all_to_all | solution.py:224
  187.1 30.3 %copy-start.196 = (pred[256]{0:T(512)(128)(4,1)}, pred[256]{0:T(512)(128)(4,1)S(1)}, u32[]{:S(2)}) copy-start(pred[256]{0:T(512)(128)(4,1)S(1)} %get-tuple-element.622) | copy-start | bytes 772
  187.1 30.3 %copy-start.198 = (pred[256]{0:T(512)(128)(4,1)}, pred[256]{0:T(512)(128)(4,1)S(1)}, u32[]{:S(2)}) copy-start(pred[256]{0:T(512)(128)(4,1)S(1)} %get-tuple-element.623) | copy-start | bytes 772
  187.1 30.3 %copy-start.200 = (pred[256]{0:T(512)(128)(4,1)}, pred[256]{0:T(512)(128)(4,1)S(1)}, u32[]{:S(2)}) copy-start(pred[256]{0:T(512)(128)(4,1)S(1)} %get-tuple-element.646) | copy-start | bytes 772
  187.2 30.3 %copy-start.202 = (pred[256]{0:T(512)(128)(4,1)}, pred[256]{0:T(512)(128)(4,1)S(1)}, u32[]{:S(2)}) copy-start(pred[256]{0:T(512)(128)(4,1)S(1)} %get-tuple-element.647) | copy-start | bytes 772
  276.6 30.2 %copy-start.7 = (f32[256,1,2,2]{3,0,2,1:T(8,128)S(1)}, f32[256,1,2,2]{3,0,2,1:T(8,128)}, u32[]{:S(2)}) copy-start(f32[256,1,2,2]{3,0,2,1:T(8,128)} %copy-done.6) | copy-start | bytes 12292
  276.6 30.3 %copy-start.5 = (f32[256,1,2,2]{3,0,2,1:T(8,128)S(1)}, f32[256,1,2,2]{3,0,2,1:T(8,128)}, u32[]{:S(2)}) copy-start(f32[256,1,2,2]{3,0,2,1:T(8,128)} %copy-done.4) | copy-start | bytes 12292
  302.8 31.3 %copy-start.126 = (f32[2,2,1]{0,1,2:T(2,128)}, f32[2,2,1]{0,1,2:T(2,128)S(1)}, u32[]{:S(2)}) copy-start(f32[2,2,1]{0,1,2:T(2,128)S(1)} %slice.3220) | copy-start | bytes 52
  306.5 27.6 %copy-start.159 = (f32[2,2,1]{0,1,2:T(2,128)}, f32[2,2,1]{0,1,2:T(2,128)S(1)}, u32[]{:S(2)}) copy-start(f32[2,2,1]{0,1,2:T(2,128)S(1)} %slice.3154) | copy-start | bytes 52
  327.9 82.4 %copy-start.88 = (f32[2,1,1,2]{3,0,2,1:T(2,128)}, f32[2,1,1,2]{3,0,2,1:T(2,128)S(1)}, u32[]{:S(2)}) copy-start(f32[2,1,1,2]{3,0,2,1:T(2,128)S(1)} %copy.2457) | copy-start | bytes 52
  328.0 82.4 %copy-start.90 = (f32[2,1,1,2]{3,0,2,1:T(2,128)}, f32[2,1,1,2]{3,0,2,1:T(2,128)S(1)}, u32[]{:S(2)}) copy-start(f32[2,1,1,2]{3,0,2,1:T(2,128)S(1)} %copy.2459) | copy-start | bytes 52
  328.0 87.2 %copy-start.92 = (f32[2,1,1,2]{3,0,2,1:T(2,128)}, f32[2,1,1,2]{3,0,2,1:T(2,128)S(1)}, u32[]{:S(2)}) copy-start(f32[2,1,1,2]{3,0,2,1:T(2,128)S(1)} %copy.2455) | copy-start | bytes 52
  378.8 15.8 %all-to-all-start.1 = ((f32[128,1,192]{2,1,0:T(1,128)}), f32[128,1,192]{2,1,0:T(1,128)S(1)}, u32[]{:S(2)}, u32[]{:S(2)}) async-start(f32[128,1,192]{2,1,0:T(1,128)} %reshape.1051), calls=%async_computation.1 | async-start | bytes 262144 | tf_op jit(solution)/shard_map/all_to_all | solution.py:228
  384.6 30.7 %copy-start.244 = (pred[32]{0:T(512)(128)(4,1)}, pred[32]{0:T(512)(128)(4,1)S(1)}, u32[]{:S(2)}) copy-start(pred[32]{0:T(512)(128)(4,1)S(1)} %get-tuple-element.654) | copy-start | bytes 100
  384.6 30.7 %copy-start.246 = (pred[32]{0:T(512)(128)(4,1)}, pred[32]{0:T(512)(128)(4,1)S(1)}, u32[]{:S(2)}) copy-start(pred[32]{0:T(512)(128)(4,1)S(1)} %get-tuple-element.655) | copy-start | bytes 100
  424.3 17.9 %all-to-all-start.2 = ((f32[2,2,2,128,8]{4,1,0,2,3:T(2,128)}), f32[2,2,2,128,8]{4,1,0,2,3:T(2,128)S(1)}, u32[]{:S(2)}, u32[]{:S(2)}) async-start(f32[2,2,2,128,8]{4,1,0,2,3:T(2,128)} %copy.2475), calls=%async_computation.2 | async-start | bytes 1048576 | tf_op jit(solution)/shard_map/all_to_all | solution.py:255
  444.2 27.8 %copy-start.221 = (f32[127,2,1]{0,1,2:T(2,128)S(1)}, f32[127,2,1]{0,1,2:T(2,128)}, u32[]{:S(2)}) copy-start(f32[127,2,1]{0,1,2:T(2,128)} %slice.3172) | copy-start | bytes 3052
  444.2 29.1 %copy-start.186 = (f32[256,2]{0,1:T(2,128)S(1)}, f32[256,2]{0,1:T(2,128)}, u32[]{:S(2)}) copy-start(f32[256,2]{0,1:T(2,128)} %get-tuple-element.248) | copy-start | bytes 6148
  444.2 29.1 %copy-start.255 = (pred[256]{0:T(512)(128)(4,1)S(1)}, pred[256]{0:T(512)(128)(4,1)}, u32[]{:S(2)}) copy-start(pred[256]{0:T(512)(128)(4,1)} %select_compare_fusion.4) | copy-start | bytes 772
  444.2 29.1 %copy-start.252 = (pred[256]{0:T(512)(128)(4,1)S(1)}, pred[256]{0:T(512)(128)(4,1)}, u32[]{:S(2)}) copy-start(pred[256]{0:T(512)(128)(4,1)} %get-tuple-element.244) | copy-start | bytes 772
  477.1 23.2 %all-to-all-start.3 = ((f32[256,2,2,1,8]{4,2,1,3,0:T(2,128)}), f32[256,2,2,1,8]{4,2,1,3,0:T(2,128)S(1)}, u32[]{:S(2)}, u32[]{:S(2)}) async-start(f32[256,2,2,1,8]{4,2,1,3,0:T(2,128)} %select_bitcast_fusion.2), calls=%async_computation.3 | async-start | bytes 1048576 | tf_op jit(solution)/shard_map/all_to_all | solution.py:257
  511.0 18.4 %all-to-all-start.4 = ((f32[2,2,2,128,8]{4,1,0,2,3:T(2,128)}), f32[2,2,2,128,8]{4,1,0,2,3:T(2,128)S(1)}, u32[]{:S(2)}, u32[]{:S(2)}) async-start(f32[2,2,2,128,8]{4,1,0,2,3:T(2,128)} %copy.2495), calls=%async_computation.4 | async-start | bytes 1048576 | tf_op jit(solution)/shard_map/all_to_all | solution.py:255
  556.6 23.1 %all-to-all-start.5 = ((f32[256,2,2,1,8]{4,1,2,3,0:T(2,128)}), f32[256,2,2,1,8]{4,1,2,3,0:T(2,128)S(1)}, u32[]{:S(2)}, u32[]{:S(2)}) async-start(f32[256,2,2,1,8]{4,1,2,3,0:T(2,128)} %copy.2505), calls=%async_computation.5 | async-start | bytes 1048576 | tf_op jit(solution)/shard_map/all_to_all | solution.py:257
  595.3 18.5 %all-to-all-start.6 = ((f32[2,2,2,128,8]{4,1,0,2,3:T(2,128)}), f32[2,2,2,128,8]{4,1,0,2,3:T(2,128)S(1)}, u32[]{:S(2)}, u32[]{:S(2)}) async-start(f32[2,2,2,128,8]{4,1,0,2,3:T(2,128)} %copy.2514), calls=%async_computation.6 | async-start | bytes 1048576 | tf_op jit(solution)/shard_map/all_to_all | solution.py:255
  (249 other events, 2853.8 us)
where the time goes:
time: 668 us; the launch traced here: 659 us
  local copies, waits for them, and re-layouts  330 us (49%)
  other arithmetic  115 us (17%)
  blocking collectives  89.7 us (13%)
  starting transfers between devices  51.4 us (8%)
  waiting for transfers between devices  48.3 us (7%)
  matrix products  16.1 us (2%)
  between operations  7.91 us (1%)
    unnamed x551, local copies, waits for them, and re-layouts  40.1 us
    all_gather x1, blocking collectives, body(): lax.all_gather(corners, 'bricks', axis=0, tiled=True)  38.2 us
    gather x18, local copies, waits for them, and re-layouts, chain_order(): pointer = jnp.take(pointer, pointer, axis=0)  35 us
    all_gather x1, blocking collectives, body(): lax.all_gather(rates, 'bricks', axis=0, tiled=True)  33.5 us
    slice x147, local copies, waits for them, and re-layouts, sorted_solve(): lax.associative_scan(compose_affine, (-f0[:, :, None], e0), reverse=True,...  31.8 us
    slice x246, local copies, waits for them, and re-layouts, sorted_solve(): summed = lax.associative_scan(compose_maps, maps, axis=0)  31.3 us
    slice x129, local copies, waits for them, and re-layouts, sorted_solve(): e1 = lax.associative_scan(compose_affine, (slope, offset), axis=0)[1]  26.4 us
    all_to_all x2, waiting for transfers between devices, solve(): lax.all_to_all(lined_jumps, 'bricks', split_axis=0, concat_axis=3, tiled=...  25.6 us
  transfers between devices with their start and end apart: 7, of which 6 were waited for; matrix products, arithmetic and copies ran while one was open for 36% of the time, Pallas kernels for 0%

commit v1 on v0

--- a/solution.py
+++ b/solution.py
@@ -3,6 +3,8 @@
 import jax
 import jax.numpy as jnp
 from jax import lax
+from jax.experimental import pallas as pl
+from jax.experimental.pallas import tpu as pltpu
 from jax.sharding import PartitionSpec as P
 
 GX = 32
@@ -12,6 +14,87 @@
 KOFF = 0.3
 BTOT = 2.0
 INFLUX = 0.1
+
+
+MESH = pl.DeviceIdType.MESH
+
+
+def exchange_kernel(n, x_ref, o_ref, land, send_sem, recv_sem, own_sem):
+    me = lax.axis_index("bricks")
+    barrier = pltpu.get_barrier_semaphore()
+
+    def greet(step, carry):
+        pl.semaphore_signal(
+            barrier, inc=1, device_id=(lax.rem(me + step, n),), device_id_type=MESH
+        )
+        return carry
+
+    lax.fori_loop(1, n, greet, 0)
+    pl.semaphore_wait(barrier, n - 1)
+
+    def send(step, carry):
+        to = lax.rem(me + step, n)
+        pltpu.make_async_remote_copy(
+            src_ref=x_ref.at[to],
+            dst_ref=land.at[me],
+            send_sem=send_sem,
+            recv_sem=recv_sem,
+            device_id=(to,),
+            device_id_type=MESH,
+        ).start()
+        return carry
+
+    lax.fori_loop(1, n, send, 0)
+    own = pltpu.make_async_copy(x_ref.at[me], land.at[me], own_sem)
+    own.start()
+    own.wait()
+    every = pltpu.make_async_remote_copy(
+        src_ref=x_ref.at[pl.ds(0, n - 1)],
+        dst_ref=land.at[pl.ds(0, n - 1)],
+        send_sem=send_sem,
+        recv_sem=recv_sem,
+        device_id=(me,),
+        device_id_type=MESH,
+    )
+    every.wait_recv()
+    every.wait_send()
+    o_ref[...] = land[...]
+
+
+def exchange(blocks):
+    n, size = blocks.shape
+    rows = 2
+    padded = jnp.pad(blocks, ((0, 0), (0, rows * 128 - size))).reshape(n, rows, 128)
+    got = pl.pallas_call(
+        partial(exchange_kernel, n),
+        out_shape=jax.ShapeDtypeStruct((n, rows, 128), jnp.float32),
+        in_specs=[pl.BlockSpec(memory_space=pltpu.VMEM)],
+        out_specs=pl.BlockSpec(memory_space=pltpu.VMEM),
+        scratch_shapes=[
+            pltpu.VMEM((n, rows, 128), jnp.float32),
+            pltpu.SemaphoreType.DMA,
+            pltpu.SemaphoreType.DMA,
+            pltpu.SemaphoreType.DMA,
+        ],
+        compiler_params=pltpu.CompilerParams(collective_id=0, has_side_effects=True),
+    )(padded)
+    return got.reshape(n, rows * 128)[:, :size]
+
+
+def to_lines(values):
+    split = values.ndim - 2
+    n = values.shape[split]
+    moved = jnp.moveaxis(values, split, 0)
+    got = exchange(moved.reshape(n, -1))
+    return got.reshape((n * values.shape[0],) + values.shape[1:split] + (1,) + values.shape[split + 1 :])
+
+
+def to_bricks(values):
+    split = values.ndim - 2
+    n = lax.axis_size("bricks")
+    got = exchange(values.reshape(n, -1))
+    shaped = got.reshape((n, values.shape[0] // n) + values.shape[1:split] + values.shape[split + 1 :])
+    return jnp.moveaxis(shaped, 0, split)
 
 
 def fetch(table, index):
@@ -221,11 +304,11 @@
     field = jnp.stack([calcium, buffer], 1).reshape(count, 2, edge, edge, edge)
     planes = end_planes(field).reshape(count, 3, 2, 2, devices, per_device)
     lined = lookup(
-        lax.all_to_all(planes, "bricks", split_axis=4, concat_axis=0, tiled=True),
+        to_lines(planes),
         neighbors[:, 0],
         neighbors[:, 1],
     )
-    halos = lax.all_to_all(lined, "bricks", split_axis=0, concat_axis=4, tiled=True).reshape(
+    halos = to_bricks(lined).reshape(
         count, 3, 2, 2, square
     )
     lams = [
@@ -252,11 +335,9 @@
             inverse_order,
         )
         lined_jumps = chain_fn(
-            lax.all_to_all(ends, "bricks", split_axis=3, concat_axis=0, tiled=True)[:, :, :, 0]
+            to_lines(ends)[:, :, :, 0]
         )[:, :, :, None]
-        jumps = lax.all_to_all(
-            lined_jumps, "bricks", split_axis=0, concat_axis=3, tiled=True
-        ).reshape(count, 2, 2, square)
+        jumps = to_bricks(lined_jumps).reshape(count, 2, 2, square)
         return correct(local, block, couple[:, d, 0], couple[:, d, 1], jumps, d)
 
     first = solve(rhs, 0)

time: 668 us -> 580 us (0.87)
  Pallas kernels: 0 us -> 105 us
  local copies, waits for them, and re-layouts: 330 us -> 274 us
  starting transfers between devices: 51.4 us -> 0 us
  waiting for transfers between devices: 48.3 us -> 0 us
  other arithmetic: 115 us -> 95.9 us
  blocking collectives: 89.7 us -> 73.6 us
    pallas_call x0 -> x8, Pallas kernels: none -> 105 us  [exchange(): pl.pallas_call(partial(exchange_kernel, n), out_shape=jax.ShapeDtypeStruc...]
    all_to_all x7 -> x0, starting transfers between devices: 51.4 us -> none  [the longest x2 19.2 us: solve(): lax.all_to_all(lined_jumps, 'bricks', split_axis=0, concat_axis=3, tiled=...]
    all_to_all x7 -> x0, waiting for transfers between devices: 48.3 us -> none  [the longest x2 25.6 us: solve(): lax.all_to_all(lined_jumps, 'bricks', split_axis=0, concat_axis=3, tiled=...]
    unnamed x551 -> x479, local copies, waits for them, and re-layouts: 40.1 us -> 17.2 us
    all_to_all x1 -> x0, blocking collectives: 18 us -> none  [solve(): lax.all_to_all(lined_jumps, 'bricks', split_axis=0, concat_axis=3, tiled=...]
    reshape x4 -> x18, local copies, waits for them, and re-layouts: 3.05 us -> 19.4 us  [the longest x8 5.91 us: exchange(): jnp.pad(blocks, ((0, 0), (0, rows * 128 - size))).reshape(n, rows, 128)]
    slice x147, local copies, waits for them, and re-layouts: 31.8 us -> 22.3 us  [sorted_solve(): lax.associative_scan(compose_affine, (-f0[:, :, None], e0), reverse=True,...]
    all_to_all x14 -> x0, local copies, waits for them, and re-layouts: 7.23 us -> none  [the longest x3 3.33 us: body(): lax.all_to_all(planes, 'bricks', split_axis=4, concat_axis=0, tiled=True)]
  transfers between devices with their start and end apart: 7 -> 0, of which waited for: 6 -> 0; matrix products, arithmetic and copies ran while one was open for 36% -> 0% of each run, Pallas kernels for 0% -> 0%
where the time goes in v1:
time: 580 us; the launch traced here: 572 us
  local copies, waits for them, and re-layouts  274 us (47%)
  Pallas kernels  105 us (18%)
  other arithmetic  95.9 us (17%)
  blocking collectives  73.6 us (13%)
  matrix products  16.1 us (3%)
  between operations  7.86 us (1%)
    pallas_call x8, Pallas kernels, exchange(): pl.pallas_call(partial(exchange_kernel, n), out_shape=jax.ShapeDtypeStruc...  105 us
    all_gather x1, blocking collectives, body(): lax.all_gather(corners, 'bricks', axis=0, tiled=True)  40 us
    gather x18, local copies, waits for them, and re-layouts, chain_order(): pointer = jnp.take(pointer, pointer, axis=0)  35.2 us
    all_gather x1, blocking collectives, body(): lax.all_gather(rates, 'bricks', axis=0, tiled=True)  33.5 us
    slice x246, local copies, waits for them, and re-layouts, sorted_solve(): summed = lax.associative_scan(compose_maps, maps, axis=0)  31.2 us
    slice x147, local copies, waits for them, and re-layouts, sorted_solve(): lax.associative_scan(compose_affine, (-f0[:, :, None], e0), reverse=True,...  22.3 us
    add x84, other arithmetic, compose_affine(): return (first_q * second_q, second_p + second_q * first_p)  21.5 us
    slice x129, local copies, waits for them, and re-layouts, sorted_solve(): e1 = lax.associative_scan(compose_affine, (slope, offset), axis=0)[1]  21.1 us

profile of v1, /device:TPU:1, one launch (start us, length us, event | category | flops | bytes accessed | tf_op | source)
XLA Modules:
  0.0 572.2 jit_solution(8345634909071055133)
XLA Ops:
  16.5 3.2 sort.92
  24.1 40.0 %all_gather.7 = f32[256,3,2,4]{1,2,0,3:T(2,128)S(1)} all-gather(f32[2,3,2,4]{1,2,0,3:T(2,128)S(1)} %pad_maximum_fusion.7), channel_id=1, replica_groups=mesh['bricks'=128] {'bricks'}, dimensions={0}, use_global_device_ids=true | all-gather | bytes 24768 | tf_op jit(solution)/shard_map/all_gather | solution.py:300
  70.2 33.5 %all_gather.6 = f32[256,3,2]{1,2,0:T(2,128)S(1)} all-gather(f32[2,3,2]{1,2,0:T(2,128)S(1)} %copy-done.24), channel_id=1, replica_groups=mesh['bricks'=128] {'bricks'}, dimensions={0}, use_global_device_ids=true | all-gather | bytes 6192 | tf_op jit(solution)/shard_map/all_gather | solution.py:299
  146.0 3.2 sort.89
  149.2 3.2 sort.90
  201.3 3.2 sort.87
  204.4 3.2 sort.88
  248.7 5.0 divide_add_fusion
  264.8 13.5 %shard_map.86 = f32[128,2,128]{2,1,0:T(2,128)} custom-call(f32[128,2,128]{2,1,0:T(2,128)} %copy.2172.x_ref), custom_call_target="tpu_custom_call" | custom-call | tf_op jit(solution)/shard_map/pallas_call | solution.py:68
  279.2 3.2 reshape.470
  287.2 3.3 fusion.51
  307.4 3.3 reshape.471
  311.4 13.0 %shard_map.87 = f32[128,2,128]{2,1,0:T(2,128)} custom-call(f32[128,2,128]{2,1,0:T(2,128)} %reshape.472.x_ref), custom_call_target="tpu_custom_call" | custom-call | tf_op jit(solution)/shard_map/pallas_call | solution.py:68
  345.4 3.8 fusion.31
  352.2 12.9 %shard_map.88 = f32[128,2,128]{2,1,0:T(2,128)} custom-call(f32[128,2,128]{2,1,0:T(2,128)} %copy.2174.x_ref), custom_call_target="tpu_custom_call" | custom-call | tf_op jit(solution)/shard_map/pallas_call | solution.py:68
  403.7 13.2 %shard_map.89 = f32[128,2,128]{2,1,0:T(2,128)} custom-call(f32[128,2,128]{2,1,0:T(2,128)} %reshape.480.x_ref), custom_call_target="tpu_custom_call" | custom-call | tf_op jit(solution)/shard_map/pallas_call | solution.py:68
  420.4 4.2 subtract_subtract_fusion.1
  424.6 3.2 fusion.25
  430.3 13.0 %shard_map.90 = f32[128,2,128]{2,1,0:T(2,128)} custom-call(f32[128,2,128]{2,1,0:T(2,128)} %copy.2178.x_ref), custom_call_target="tpu_custom_call" | custom-call | tf_op jit(solution)/shard_map/pallas_call | solution.py:68
  482.6 12.9 %shard_map.91 = f32[128,2,128]{2,1,0:T(2,128)} custom-call(f32[128,2,128]{2,1,0:T(2,128)} %reshape.487.x_ref), custom_call_target="tpu_custom_call" | custom-call | tf_op jit(solution)/shard_map/pallas_call | solution.py:68
  497.7 3.7 subtract_subtract_fusion
  501.4 9.1 %fusion.23 = f32[2,2,32,32,32]{3,4,2,1,0:T(8,128)S(1)} fusion(f32[2,2,32,32,32]{4,2,3,1,0:T(8,128)S(1)} %subtract_subtract_fusion, f32[2,3,2,32,32]{4,3,2,1,0:T(8,128)S(1)} %copy-done.8), kind=kOutput, calls=%fused_computation.78 | convolution fusion | flops 50331648 | bytes 2686976 | tf_op jit(solution)/shard_map/psab,psijb->psija/dot_general | solution.py:163
  512.2 13.2 %shard_map.92 = f32[128,2,128]{2,1,0:T(2,128)} custom-call(f32[128,2,128]{2,1,0:T(2,128)} %copy.2182.x_ref), custom_call_target="tpu_custom_call" | custom-call | tf_op jit(solution)/shard_map/pallas_call | solution.py:68
  551.5 13.0 %shard_map.93 = f32[128,2,128]{2,1,0:T(2,128)} custom-call(f32[128,2,128]{2,1,0:T(2,128)} %reshape.494.x_ref), custom_call_target="tpu_custom_call" | custom-call | tf_op jit(solution)/shard_map/pallas_call | solution.py:68
  (2067 shorter events, 331.6 us)
Async XLA Ops:
  20.2 88.4 %copy-start.31 = (s32[1024]{0:T(1024)}, s32[1024]{0:T(1024)S(1)}, u32[]{:S(2)}) copy-start(s32[1024]{0:T(1024)S(1)} %pad_clamp_fusion.1) | copy-start | bytes 12292
  22.7 86.7 %copy-start.36 = (pred[256]{0:T(512)(128)(4,1)}, pred[256]{0:T(512)(128)(4,1)S(1)}, u32[]{:S(2)}) copy-start(pred[256]{0:T(512)(128)(4,1)S(1)} %get-tuple-element.41) | copy-start | bytes 772
  110.0 31.8 %copy-start.14 = (f32[256,2]{0,1:T(2,128)}, f32[256,2]{0,1:T(2,128)S(1)}, u32[]{:S(2)}) copy-start(f32[256,2]{0,1:T(2,128)S(1)} %get-tuple-element.402) | copy-start | bytes 6148
  110.1 31.8 %copy-start.16 = (f32[256,2]{0,1:T(2,128)}, f32[256,2]{0,1:T(2,128)S(1)}, u32[]{:S(2)}) copy-start(f32[256,2]{0,1:T(2,128)S(1)} %get-tuple-element.403) | copy-start | bytes 6148
  163.2 31.8 %copy-start.18 = (f32[256,2]{0,1:T(2,128)}, f32[256,2]{0,1:T(2,128)S(1)}, u32[]{:S(2)}) copy-start(f32[256,2]{0,1:T(2,128)S(1)} %get-tuple-element.406) | copy-start | bytes 6148
  163.3 31.8 %copy-start.20 = (f32[256,2]{0,1:T(2,128)}, f32[256,2]{0,1:T(2,128)S(1)}, u32[]{:S(2)}) copy-start(f32[256,2]{0,1:T(2,128)S(1)} %get-tuple-element.407) | copy-start | bytes 6148
  216.6 28.5 %copy-start.11 = (f32[2,32,1024]{2,1,0:T(8,128)S(1)}, f32[2,32,1024]{2,1,0:T(8,128)}, u32[]{:S(2)}) copy-start(f32[2,32,1024]{2,1,0:T(8,128)} %param.18) | copy-start | bytes 786436
  217.4 28.1 %copy-start.12 = (f32[2,32,1024]{2,1,0:T(8,128)S(1)}, f32[2,32,1024]{2,1,0:T(8,128)}, u32[]{:S(2)}) copy-start(f32[2,32,1024]{2,1,0:T(8,128)} %param.19) | copy-start | bytes 786436
  218.2 29.1 %copy-start.22 = (f32[256,2]{0,1:T(2,128)}, f32[256,2]{0,1:T(2,128)S(1)}, u32[]{:S(2)}) copy-start(f32[256,2]{0,1:T(2,128)S(1)} %get-tuple-element.411) | copy-start | bytes 6148
  245.0 91.2 %copy-start.126 = (f32[2,1,1,2]{3,0,2,1:T(2,128)}, f32[2,1,1,2]{3,0,2,1:T(2,128)S(1)}, u32[]{:S(2)}) copy-start(f32[2,1,1,2]{3,0,2,1:T(2,128)S(1)} %copy.2101) | copy-start | bytes 52
  245.1 91.2 %copy-start.128 = (f32[2,1,1,2]{3,0,2,1:T(2,128)}, f32[2,1,1,2]{3,0,2,1:T(2,128)S(1)}, u32[]{:S(2)}) copy-start(f32[2,1,1,2]{3,0,2,1:T(2,128)S(1)} %copy.2103) | copy-start | bytes 52
  352.2 27.5 %copy-start.106 = (f32[128,2,1]{0,1,2:T(2,128)S(1)}, f32[128,2,1]{0,1,2:T(2,128)}, u32[]{:S(2)}) copy-start(f32[128,2,1]{0,1,2:T(2,128)} %copy-done.105) | copy-start | bytes 3076
  352.2 28.2 %copy-start.125 = (f32[256,2,1]{0,1,2:T(2,128)S(1)}, f32[256,2,1]{0,1,2:T(2,128)}, u32[]{:S(2)}) copy-start(f32[256,2,1]{0,1,2:T(2,128)} %copy-done.124) | copy-start | bytes 6148
  368.2 27.4 %copy-start.123 = (f32[256,2,1]{0,1,2:T(2,128)S(1)}, f32[256,2,1]{0,1,2:T(2,128)}, u32[]{:S(2)}) copy-start(f32[256,2,1]{0,1,2:T(2,128)} %copy-done.122) | copy-start | bytes 6148
  371.1 28.3 %copy-start.42 = (pred[256]{0:T(512)(128)(4,1)S(1)}, pred[256]{0:T(512)(128)(4,1)}, u32[]{:S(2)}) copy-start(pred[256]{0:T(512)(128)(4,1)} %copy-done.40) | copy-start | bytes 772
  371.2 28.3 %copy-start.204 = (f32[256,2]{0,1:T(2,128)S(1)}, f32[256,2]{0,1:T(2,128)}, u32[]{:S(2)}) copy-start(f32[256,2]{0,1:T(2,128)} %get-tuple-element.248) | copy-start | bytes 6148
  429.6 27.8 %copy-start.88 = (f32[64,2,1]{0,1,2:T(2,128)S(1)}, f32[64,2,1]{0,1,2:T(2,128)}, u32[]{:S(2)}) copy-start(f32[64,2,1]{0,1,2:T(2,128)} %copy-done.87) | copy-start | bytes 1540
  430.3 28.1 %copy-start.86 = (f32[128,2,1]{0,1,2:T(2,128)S(1)}, f32[128,2,1]{0,1,2:T(2,128)}, u32[]{:S(2)}) copy-start(f32[128,2,1]{0,1,2:T(2,128)} %copy-done.85) | copy-start | bytes 3076
  445.0 27.4 %copy-start.80 = (f32[32,2,1]{0,1,2:T(2,128)S(1)}, f32[32,2,1]{0,1,2:T(2,128)}, u32[]{:S(2)}) copy-start(f32[32,2,1]{0,1,2:T(2,128)} %copy-done.79) | copy-start | bytes 772
  445.0 27.9 %copy-start.78 = (f32[64,2,1]{0,1,2:T(2,128)S(1)}, f32[64,2,1]{0,1,2:T(2,128)}, u32[]{:S(2)}) copy-start(f32[64,2,1]{0,1,2:T(2,128)} %copy-done.77) | copy-start | bytes 1540
  445.0 29.0 %copy-start.76 = (f32[128,2,1]{0,1,2:T(2,128)S(1)}, f32[128,2,1]{0,1,2:T(2,128)}, u32[]{:S(2)}) copy-start(f32[128,2,1]{0,1,2:T(2,128)} %copy-done.75) | copy-start | bytes 3076
  445.1 30.1 %copy-start.120 = (f32[256,2,1]{0,1,2:T(2,128)S(1)}, f32[256,2,1]{0,1,2:T(2,128)}, u32[]{:S(2)}) copy-start(f32[256,2,1]{0,1,2:T(2,128)} %copy-done.119) | copy-start | bytes 6148
  449.2 29.8 %copy-start.203 = (f32[256,2]{0,1:T(2,128)S(1)}, f32[256,2]{0,1:T(2,128)}, u32[]{:S(2)}) copy-start(f32[256,2]{0,1:T(2,128)} %get-tuple-element.146) | copy-start | bytes 6148
  451.0 28.1 %copy-start.225 = (pred[256]{0:T(512)(128)(4,1)S(1)}, pred[256]{0:T(512)(128)(4,1)}, u32[]{:S(2)}) copy-start(pred[256]{0:T(512)(128)(4,1)} %get-tuple-element.142) | copy-start | bytes 772
  (206 other events, 2348.6 us)

commit v2 on v0

v2 whole, which is shorter than its diff:
```python
import jax
import jax.numpy as jnp
from jax import lax
from jax.experimental import pallas as pl
from jax.experimental.pallas import tpu as pltpu
from jax.sharding import PartitionSpec as P

KON = 0.5
KOFF = 0.3
BTOT = 2.0
INFLUX = 0.1

MESH = pl.DeviceIdType.MESH
F32 = jnp.float32
BF16 = jnp.bfloat16
HIGH = lax.Precision.HIGHEST
N = 128
E = 32
OWNERS = 64


def iota(shape, axis):
    return lax.broadcasted_iota(jnp.int32, shape, axis)


def roll(x, shift, axis=-1):
    if axis < 0:
        axis += x.ndim
    if isinstance(shift, int):
        shift %= x.shape[axis]
        if shift == 0:
            return x
    return pltpu.roll(x, shift, axis)


def rho_of(r):
    h = 0.5 / r
    s = jnp.sqrt(h * (2.0 + h))
    return 1.0 + h - s, s - h


def power(log_rho, n):
    return jnp.exp(log_rho * n.astype(F32))


def corners(r):
    rho, gap = rho_of(r)
    p2 = rho * rho
    p4 = p2 * p2
    p8 = p4 * p4
    p16 = p8 * p8
    p32 = p16 * p16
    kappa = rho / (r * gap * (1.0 - p32 * p32))
    return kappa * (1.0 + p32 * p32 / rho), kappa * (p32 / rho + p32)


def column(r, index):
    rho, gap = rho_of(r)
    lr = jnp.log(rho)
    kappa = rho / (r * gap * (1.0 - jnp.exp(lr * 64.0)))
    return kappa * (power(lr, index) + power(lr, 63 - index))


def inverse_blocks(r):
    rho, gap = rho_of(r)
    lr = jnp.log(rho)
    scale = rho / (r * gap * (1.0 + rho) * (1.0 - jnp.exp(lr * 64.0)))
    row, col = iota((N, N), 0), iota((N, N), 1)
    a, b = row & 31, col & 31
    away = jnp.abs(a - b)
    total = power(lr, away) + power(lr, a + b + 1) + power(lr, 63 - a - b) + power(lr, 64 - away)
    return jnp.where((row >> 5) == (col >> 5), total * scale, 0.0)


def sweep_terms(r, index):
    rho, _ = rho_of(r)
    lr = jnp.log(rho)
    rho2 = rho * rho
    odd = power(lr, 2 * index + 1)
    ratio = rho * (1.0 + odd) / (1.0 + odd * rho2)
    last = jnp.exp(lr * 61.0)
    ratio30 = rho * (1.0 + last) / (1.0 + last * rho2)
    m = jnp.where(index == E - 1, 1.0 / (1.0 + r - r * ratio30), ratio / r)
    return m, m * r


def swap_blocks(x, grp):
    low = grp < 2
    even = (grp & 1) == 0
    y = [None] * 4
    for q in range(2):
        a, b = x[q], x[q + 2]
        y[q] = jnp.where(low, a, roll(b, 64))
        y[q + 2] = jnp.where(low, roll(a, 64), b)
    z = [None] * 4
    for q in (0, 2):
        a, b = y[q], y[q + 1]
        z[q] = jnp.where(even, a, roll(b, 32))
        z[q + 1] = jnp.where(even, roll(a, -32), b)
    return z


def split3(x):
    a = x.astype(BF16)
    rest = x - a.astype(F32)
    b = rest.astype(BF16)
    c = (rest - b.astype(F32)).astype(BF16)
    return a, b, c


def pick(select, x):
    out = None
    for part in split3(x):
        term = jnp.dot(select, part, preferred_element_type=F32)
        out = term if out is None else out + term
    return out


def pick_right(x, select):
    out = None
    for part in split3(x):
        term = jnp.dot(part, select, preferred_element_type=F32)
        out = term if out is None else out + term
    return out


def dot(a, b):
    return jnp.dot(a, b, precision=HIGH, preferred_element_type=F32)


def dot_first(a, b):
    return lax.dot_general(
        a, b, (((0,), (0,)), ((), ())), precision=HIGH, preferred_element_type=F32
    )


def one_hot(cond):
    return jnp.where(cond, 1.0, 0.0).astype(BF16)


def total(x, axis):
    return jnp.sum(x, axis=axis, keepdims=True)


def step_kernel(
    rates, nbs, nbv, rkv, cal, buf, frac, out_c, out_b,
    u_ref, f_ref, t_ref, g_ref, msg0, rt, send1, land1, send2, land2,
    co0, co1, ecm, ece, e_ref, pl_ref, perm, permt, kk, chain,
    ss0, rs0, ss1, rs1, ss2, rs2, own_sem,
):
    me = lax.axis_index("bricks")
    barrier = pltpu.get_barrier_semaphore()

    def greet(step, carry):
        pl.semaphore_signal(
            barrier, inc=1, device_id=(lax.rem(me + step, N),), device_id_type=MESH
        )
        return carry

    lax.fori_loop(1, N, greet, 0)

    lane = iota((1, N), 1)
    lane32 = lane & 31
    grp = lane >> 5
    sub8 = iota((8, N), 0)
    row32 = iota((E, N), 0)

    own = []
    for d in range(3):
        r = jnp.zeros((1, N), F32)
        for q in range(4):
            r = jnp.where(grp == q, rates[q // 2, d, q % 2], r)
        own.append(r)
    message = jnp.where(lane32 == 0, own[0], jnp.where(lane32 == 1, own[1], own[2]))
    msg0[0] = message
    near = {}
    for name, d, side in (("yl", 1, 0), ("yu", 1, 1), ("zl", 2, 0), ("zu", 2, 1)):
        near[name] = [nbs[d, side, 2 * me + b] for b in range(2)]
    near["z"] = [jnp.maximum(near["zl"][b], near["zu"][b]) for b in range(2)]

    def by_brick(pair):
        return jnp.where(lane < 64, pair[0], pair[1])

    up = by_brick([jnp.where(v >= 0, 1, 0) for v in near["zu"]]) == 1
    upf = jnp.where(up, 1.0, 0.0)
    face_lane = lane32 == jnp.where(up, E - 1, 0)

    def lay(t, carry):
        cols = pl.ds(pl.multiple_of(t * N, N), N)
        us, fs = [], []
        for b in range(2):
            ca, bo, al = cal[b, :, cols], buf[b, :, cols], frac[b, :, cols]
            bind = KON * ca * (BTOT - bo) - KOFF * bo
            us += [ca, bo]
            fs += [2.0 * ca - bind + INFLUX * (1.0 - al) / al, 2.0 * bo + bind]
        us = swap_blocks(us, grp)
        fs = swap_blocks(fs, grp)
        for m in range(4):
            at = pl.ds(pl.multiple_of((t * 4 + m) * E, E), E)
            u_ref[at, :] = us[m]
            f_ref[at, :] = fs[m]
        return carry

    lax.fori_loop(0, 8, lay, 0)

    m, e = sweep_terms(own[0], row32)
    co0[0] = m
    co0[1] = e
    m, e = sweep_terms(own[1], row32)
    co1[0] = m
    co1[1] = e

    pl.semaphore_wait(barrier, N - 1)

    def send_rates(step, carry):
        to = lax.rem(me + step, N)
        pltpu.make_async_remote_copy(
            msg0, rt.at[pl.ds(me, 1)], ss0, rs0, device_id=(to,), device_id_type=MESH
        ).start()
        return carry

    lax.fori_loop(1, N, send_rates, 0)
    keep = pltpu.make_async_copy(msg0, rt.at[pl.ds(me, 1)], own_sem.at[0])
    keep.start()

    def face(j, plane):
        u = u_ref[pl.ds(pl.multiple_of(j * E, E), E), :]
        first = roll(u, j)
        last = roll(u, j + (N - E + 1))
        return jnp.where(lane32 == j, jnp.where(up, last, first), plane)

    wz = lax.fori_loop(0, E, face, jnp.zeros((E, N), F32))

    owner = lax.rem(me, 2) == 0

    @pl.when(owner)
    def _():
        s2, l2 = iota((256, 256), 0), iota((256, 256), 1)
        lane256 = iota((1, 256), 1)

        def heads(before, doublings):
            target = jnp.where(before < 0, lane256, before)
            step = one_hot(s2 == target)
            for _ in range(doublings):
                step = jnp.dot(step, step, preferred_element_type=F32).astype(BF16)
            return step

        before0, before1 = nbv[0, 0:1, :], nbv[1, 0:1, :]
        znear = jnp.maximum(nbv[2, 0:1, :], nbv[2, 1:2, :]).astype(F32)
        rank0, rank1 = rkv[0:1, :].astype(F32), rkv[1:2, :].astype(F32)
        lead = jnp.dot(heads(before1, 3), heads(before0, 5), preferred_element_type=F32)
        key = total(lead * s2.astype(F32), 0) * 32.0 + rank1
        keyed = total(jnp.where(s2 == l2, key + rank0 * 1e5, 0.0), 1)
        row = total(jnp.where(keyed < key, 1.0, 0.0), 0)
        pos = rank0 * 8.0 + row
        at = s2.astype(F32) == pos
        slot_at = total(jnp.where(at, lane256.astype(F32), 0.0), 1)
        rank_at = total(jnp.where(at, rank1, 0.0), 1)
        z_at = total(jnp.where(at, znear, 0.0), 1)
        kk[0] = jnp.where(rank_at > 0.5, 1.0, jnp.zeros((256, N), F32))
        dev = lane.astype(F32) * 2.0
        s1, l1 = iota((N, 256), 0), iota((N, 256), 1)
        lf = l1.astype(F32)
        for b in range(2):
            perm[b] = one_hot(slot_at == dev + b)
            perm[2 + b] = one_hot(z_at == dev + b)
            mine = l1 == 2 * s1 + b
            pos_b = total(jnp.where(mine, pos, 0.0), 1)
            z_b = total(jnp.where(mine, znear, 0.0), 1)
            posz_b = total(jnp.where(lf == z_b, pos + 1.0, 0.0), 1) - 1.0
            permt[b] = one_hot(lf == pos_b)
            permt[2 + b] = one_hot(lf == posz_b)

    keep.wait()
    arrive = pltpu.make_async_remote_copy(
        rt.at[pl.ds(0, N - 1)], rt.at[pl.ds(0, N - 1)], ss0, rs0, device_id=(me,), device_id_type=MESH
    )
    arrive.wait_recv()

    def rates_of(indices):
        rows = []
        for b in range(2):
            index = jnp.maximum(indices[b], 0)
            got = rt[index >> 1]
            cross = (index & 1) != b
            rows.append(jnp.where(cross, roll(got, 64), got))
        got = jnp.where(lane < 64, rows[0], rows[1])
        has = by_brick([jnp.where(indices[b] >= 0, 1.0, 0.0) for b in range(2)])
        return got, has

    stack = jnp.ones((8, N), F32)
    has = jnp.zeros((8, N), F32)
    for at, name in ((0, "yu"), (1, "yl"), (2, "z")):
        got, there = rates_of(near[name])
        stack = jnp.where(sub8 == at, got, stack)
        has = jnp.where(sub8 == at, there, has)
    stack = jnp.where(sub8 == 3, message, stack)
    near_r = []
    for d in range(3):
        x = roll(jnp.where(lane32 == d, stack, 0.0), -d)
        for shift in (1, 2, 4, 8, 16):
            x = x + roll(x, shift)
        near_r.append(x)
    g1 = has * 2.0 * own[1] * near_r[1] / (own[1] + near_r[1])
    g2 = has * 2.0 * own[2] * near_r[2] / (own[2] + near_r[2])
    gyu, gyl, gz = g1[0:1], g1[1:2], g2[2:3]

    cu2 = jnp.where(lane32 < E - 1, 2.0 * own[2], 0.0)
    cd2 = jnp.where(lane32 > 0, 2.0 * own[2], 0.0)
    dg2 = cu2 + cd2 + jnp.where(face_lane, 2.0 * gz, 0.0)
    r1x2 = 2.0 * own[1]

    def right_side(j, prev):
        at = pl.ds(pl.multiple_of(j * E, E), E)
        u = u_ref[at, :]
        nxt = u_ref[pl.ds(pl.multiple_of(jnp.minimum(j + 1, E - 1) * E, E), E), :]
        low = jnp.where(j == 0, 0.0, r1x2)
        high = jnp.where(j == E - 1, 0.0, r1x2)
        out_low = jnp.where(j == 0, 2.0 * gyl, r1x2)
        out_high = jnp.where(j == E - 1, 2.0 * gyu, r1x2)
        f_ref[at, :] = (
            f_ref[at, :]
            + cu2 * roll(u, -1)
            + cd2 * roll(u, 1)
            + low * prev
            + high * nxt
            - (dg2 + out_low + out_high) * u
        )
        return u

    lax.fori_loop(0, E, right_side, jnp.zeros((E, N), F32))

    u_first, u_last = u_ref[0:E, :], u_ref[(E - 1) * E : E * E, :]
    s_up = 2.0 * gyu * u_last
    s_low = 2.0 * gyl * u_first
    s_z = 2.0 * gz * wz

    i8 = iota((E, 8, N), 0)
    mm, ee = sweep_terms(near_r[0][None], i8)
    ecm[...] = mm
    ece[...] = ee

    def solve_i(load_plane_row):
        def forward(i, carry):
            g, h = carry
            at = pl.ds(i, E, stride=E)
            g = co0[0, pl.ds(i, 1), :] * f_ref[at, :] + co0[1, pl.ds(i, 1), :] * g
            t_ref[at, :] = g
            h = ecm[i] * load_plane_row(i) + ece[i] * h
            e_ref[i] = h
            return g, h

        g, h = lax.fori_loop(0, E, forward, (jnp.zeros((E, N), F32), jnp.zeros((8, N), F32)))

        def backward(step, carry):
            i = E - 2 - step
            x, h = carry
            at = pl.ds(i, E, stride=E)
            x = t_ref[at, :] + co0[1, pl.ds(i, 1), :] * x
            t_ref[at, :] = x
            h = e_ref[i] + ece[i] * h
            e_ref[i] = h
            return x, h

        lax.fori_loop(0, E - 1, backward, (g, h))

    def solve_j(extra_first, extra_last):
        def forward(j, g):
            at = pl.ds(pl.multiple_of(j * E, E), E)
            d = t_ref[at, :] - 2.0 * u_ref[at, :]
            if extra_first is not None:
                d = d + jnp.where(j == 0, extra_first, 0.0) + jnp.where(j == E - 1, extra_last, 0.0)
            g = co1[0, pl.ds(j, 1), :] * d + co1[1, pl.ds(j, 1), :] * g
            g_ref[at, :] = g
            return g

        g = lax.fori_loop(0, E, forward, jnp.zeros((E, N), F32))

        def backward(step, x):
            j = E - 2 - step
            at = pl.ds(pl.multiple_of(j * E, E), E)
            x = g_ref[at, :] + co1[1, pl.ds(j, 1), :] * x
            g_ref[at, :] = x
            return x

        lax.fori_loop(0, E - 1, backward, g)

    pl_ref[0] = s_up
    pl_ref[1] = s_low
    pl_ref[2] = s_z

    def first_rows(i):
        x = jnp.where(sub8 == 0, pl_ref[0, pl.ds(i, 1), :], 0.0)
        x = jnp.where(sub8 == 1, pl_ref[1, pl.ds(i, 1), :], x)
        return jnp.where(sub8 == 2, pl_ref[2, pl.ds(i, 1), :], x)

    solve_i(first_rows)
    for p in range(3):
        pl_ref[p] = e_ref[:, p, :]
    solve_j(None, None)

    rowN, colN = iota((N, N), 0), iota((N, N), 1)
    kin = rowN & 31
    weight = column(own[2], jnp.where(up, E - 1 - kin, kin))
    weight = jnp.where((rowN >> 5) == (colN >> 5), weight, 0.0)

    def face_mean(j, plane):
        y = g_ref[pl.ds(pl.multiple_of(j * E, E), E), :]
        return jnp.where(lane32 == j, dot(y, weight), plane)

    t_own = lax.fori_loop(0, E, face_mean, jnp.zeros((E, N), F32))

    y0f = t_ref[pl.ds(0, E, stride=E), :]
    y0l = t_ref[pl.ds(E - 1, E, stride=E), :]
    y1f, y1l = g_ref[0:E, :], g_ref[(E - 1) * E : E * E, :]
    rows_a = jnp.transpose(jnp.concatenate([y0f, y0l, y1f, y1l], 0))
    rows_b = jnp.transpose(jnp.concatenate([s_up, s_low, pl_ref[0], pl_ref[1]], 0))
    pz = pl_ref[2]
    v1z = column(near_r[1][2:3], lane32)
    w1z = column(near_r[1][2:3], E - 1 - lane32)
    ends = jnp.where(
        (sub8 & 3) == grp, jnp.where(sub8 < 4, v1z, w1z), 0.0
    )
    ends_i = lax.dot_general(
        ends, pz, (((1,), (1,)), ((), ())), precision=HIGH, preferred_element_type=F32
    )
    ends_i = jnp.concatenate([ends_i, jnp.zeros((8, N - E), F32)], 1)
    for q in range(4):
        b, sp = q // 2, q % 2
        base = sp * 8 + b * 4
        send1[pl.ds(base, E, stride=16), :] = rows_a[q * E : (q + 1) * E]
        send1[pl.ds(base + 1, E, stride=16), :] = rows_b[q * E : (q + 1) * E]
        c = jnp.where(lane < 32, roll(pz[0:1], -E * q), roll(pz[E - 1 : E], E - E * q))
        c = jnp.where(lane < 64, c, roll(ends_i[q : q + 1], 64))
        c = jnp.where(lane < 96, c, roll(ends_i[q + 4 : q + 5], 96))
        kf = jnp.where(near["zu"][b] >= 0, 0, E - 1)
        send1[pl.ds(base + 2, E, stride=16), :] = jnp.where(row32 == kf, c, 0.0)
        dd = jnp.where(
            lane < 32, roll(s_z, -E * q), jnp.where(lane < 64, roll(t_own, E - E * q), 0.0)
        )
        send1[pl.ds(base + 3, E, stride=16), :] = roll(dd, 64)

    def block(ref, index):
        return ref.at[pl.ds(pl.multiple_of(index * 8, 8), 8)]

    mine = me // 2

    def send_ends(step, carry):
        o = lax.rem(mine + step, OWNERS)
        pltpu.make_async_remote_copy(
            block(send1, o), block(land1, me), ss1, rs1, device_id=(2 * o,), device_id_type=MESH
        ).start()
        return carry

    lax.fori_loop(1, OWNERS, send_ends, 0)

    @pl.when(jnp.logical_not(owner))
    def _():
        pltpu.make_async_remote_copy(
            block(send1, mine), block(land1, me), ss1, rs1, device_id=(2 * mine,), device_id_type=MESH
        ).start()

    @pl.when(owner)
    def _():
        local = pltpu.make_async_copy(block(send1, mine), block(land1, me), own_sem.at[1])
        local.start()
        sp32 = lax.rem(mine, 2) * 32
        table = rt[:, 0, :]
        ordered = pick(perm[0], table) + pick(perm[1], roll(table, 64))
        pick_at = iota((N, 2 * N), 0)
        pick_to = iota((N, 2 * N), 1) >> 7
        both = pick_right(ordered, one_hot(pick_at == sp32 + pick_to))
        r0, r1 = both[:, 0:N], both[:, N : 2 * N]
        p256 = iota((256, N), 0)
        linked = kk[0]
        dims = []
        for d, r in ((0, r0), (1, r1)):
            alpha, eps = corners(r)
            if d == 0:
                before = jnp.concatenate([r[0:8], r[0:248]], 0)
                gl = jnp.where(p256 >= 8, 2.0 * r * before / (r + before), 0.0)
                gr = jnp.concatenate([gl[8:256], jnp.zeros((8, N), F32)], 0)
            else:
                before = roll(r, 1, 0)
                gl = linked * 2.0 * r * before / (r + before)
                gr = roll(gl, -1, 0)
            dims.append((alpha, eps, gl, gr))
            chain[0 + 4 * d] = alpha
            chain[1 + 4 * d] = eps
            chain[2 + 4 * d] = gl
            chain[3 + 4 * d] = gr

        def elimination(alpha, eps, gl, gr, fq):
            b00 = 1.0 + gl * alpha * (1.0 + fq)
            b10 = gl * eps * (1.0 + fq)
            det = b00 * (1.0 + gr * alpha) - gr * eps * b10
            return b00, b10, 1.0 / det

        def along(x, fq):
            at = pl.ds(pl.multiple_of(x * 8, 8), 8)
            alpha, eps, gl, gr = [chain[c, at, :] for c in range(4)]
            kk[1, at, :] = fq
            b00, b10, inv = elimination(alpha, eps, gl, gr, fq)
            return -gr * (b00 * alpha - b10 * eps) * inv

        lax.fori_loop(0, E, along, jnp.zeros((8, N), F32))
        alpha, eps, gl, gr = dims[1]
        fq = jnp.zeros((256, N), F32)
        for _ in range(7):
            b00, b10, inv = elimination(alpha, eps, gl, gr, fq)
            fq = linked * roll(-gr * (b00 * alpha - b10 * eps) * inv, 1, 0)
        kk[2] = fq

        def terms(d, fq):
            alpha, eps, gl, gr = [chain[4 * d + c] for c in range(4)]
            b00, b10, inv = elimination(alpha, eps, gl, gr, fq)
            a01, a11 = gr * eps, 1.0 + gr * alpha
            base = 3 + 8 * d
            kk[base] = b00 * inv
            kk[base + 1] = -b10 * inv
            kk[base + 2] = a11 * inv
            kk[base + 3] = -a01 * inv
            kk[base + 4] = gl * (a11 * alpha - a01 * eps) * inv
            kk[base + 5] = -gr * (b00 * alpha - b10 * eps) * inv
            kk[base + 6] = gl * (b00 * eps - b10 * alpha) * inv
            kk[base + 7] = gr * eps * inv

        terms(0, kk[1])
        terms(1, kk[2])
        both_l = lane32 + 0 * p256
        j_of = jnp.where((grp & 1) == 0, both_l, E - 1 - both_l)
        chain[8] = column(r1, j_of)
        chain[9] = column(r0, both_l)
        chain[10] = column(r0, E - 1 - both_l)
        local.wait()
        got = pltpu.make_async_remote_copy(
            land1.at[pl.ds(0, 8 * (N - 1))], land1.at[pl.ds(0, 8 * (N - 1))], ss1, rs1,
            device_id=(me,), device_id_type=MESH,
        )
        got.wait_recv()

        def ordered_rows(kind, which):
            return pick(perm[which], land1[pl.ds(kind, N, stride=8), :]) + pick(
                perm[which + 1], land1[pl.ds(4 + kind, N, stride=8), :]
            )

        link_next = roll(kk[0], -1, 0)
        ya = ordered_rows(0, 0) + ordered_rows(2, 2)
        yb = ordered_rows(1, 0)
        yd = ordered_rows(3, 0)
        bl = kk[0] * roll(yb, 1, 0)
        bu = link_next * roll(yb, -1, 0)
        out2 = jnp.where(lane < 32, bl, jnp.where(lane < 64, bu, yd))
        straight = jnp.where(lane < 96, bl, bu)
        crossed = jnp.where(lane < 96, roll(bu, -32), roll(bl, 32))
        ya = ya + jnp.where(lane >= 64, chain[4] * straight + chain[5] * crossed, 0.0)
        ya = ya + jnp.where(lane == 0, roll(bl, 64), 0.0) + jnp.where(lane == 32, roll(bl, 65), 0.0)
        ya = ya + jnp.where(lane == 31, roll(bu, 63), 0.0) + jnp.where(lane == 63, roll(bu, 64), 0.0)

        def before_x(v, n):
            return jnp.concatenate([jnp.zeros((8 * n, N), F32), v[0 : 256 - 8 * n]], 0)

        def after_x(v, n):
            return jnp.concatenate([v[8 * n : 256], jnp.zeros((8 * n, N), F32)], 0)

        def before_y(v, n):
            return roll(v, n, 0)

        def after_y(v, n):
            return roll(v, -n, 0)

        def chains(y0, y1, d, gl, gr, before, after, steps):
            base = 3 + 8 * d
            e1 = kk[base] * y1 + kk[base + 1] * y0
            slope = kk[base + 6]
            for n in steps:
                e1 = e1 + slope * before(e1, n)
                slope = slope * before(slope, n)
            e0 = kk[base + 2] * y0 + kk[base + 3] * y1 + kk[base + 4] * before(e1, 1)
            slope = kk[base + 7]
            zp = e0
            for n in steps:
                zp = zp + slope * after(zp, n)
                slope = slope * after(slope, n)
            zp_next = after(zp, 1)
            zq = e1 + -kk[base + 5] * zp_next
            return -gl * (zp - before(zq, 1)), -gr * (zq - zp_next)

        al, ar = chains(
            ya, roll(ya, -32), 0, chain[2], chain[3], before_x, after_x, (1, 2, 4, 8, 16)
        )
        spread = jnp.where(
            lane < 64,
            jnp.where(lane < 32, al, roll(al, 32)),
            jnp.where(lane < 96, roll(ar, 64), roll(ar, 96)),
        )
        src = iota((N, 2 * N), 0) >> 5
        dst = iota((N, 2 * N), 1)
        side, part = dst >> 7, (dst >> 5) & 3
        sums = pick_right(
            spread * chain[8], one_hot((part >= 2) & (src == 2 * side + part - 2))
        )
        ya = ya + chain[9] * sums[:, 0:N] + chain[10] * sums[:, N : 2 * N]
        bl_c, br_c = chains(ya, roll(ya, -32), 1, chain[6], chain[7], before_y, after_y, (1, 2, 4))
        out1 = jnp.where(
            lane < 64,
            jnp.where(lane < 32, al, roll(ar, 32)),
            jnp.where(lane < 96, bl_c, roll(br_c, 32)),
        )
        for b in range(2):
            for kind, which, what in ((0, b, out1), (1, b, out2), (2, 2 + b, out1), (3, 2 + b, out2)):
                send2[pl.ds(b * 4 + kind, N, stride=8), :] = pick(permt[which], what)

        def send_back(step, carry):
            to = lax.rem(me + step, N)
            pltpu.make_async_remote_copy(
                block(send2, to), block(land2, mine), ss2, rs2, device_id=(to,), device_id_type=MESH
            ).start()
            return carry

        lax.fori_loop(1, N, send_back, 0)
        local = pltpu.make_async_copy(block(send2, me), block(land2, mine), own_sem.at[2])
        local.start()
        local.wait()

    def arrived2(count):
        part = land2.at[pl.ds(0, 8 * count)]
        pltpu.make_async_remote_copy(
            part, part, ss2, rs2, device_id=(me,), device_id_type=MESH
        ).wait_recv()

    @pl.when(owner)
    def _():
        arrived2(OWNERS - 1)

    @pl.when(jnp.logical_not(owner))
    def _():
        arrived2(OWNERS)

    def gathered(kind):
        return jnp.concatenate(
            [land2[pl.ds((q % 2) * 8 + (q // 2) * 4 + kind, E, stride=16), :] for q in range(4)], 0
        )

    own_ab, own_h, near_ab, near_h = [gathered(kind) for kind in range(4)]
    ab = jnp.transpose(own_ab)
    halo = jnp.transpose(own_h)
    w_near = jnp.zeros((E, N), F32)
    t_near = jnp.zeros((E, N), F32)
    for q in range(4):
        part = near_h[q * E : (q + 1) * E]
        w_near = jnp.where(grp == q, roll(part, E * q - 64), w_near)
        t_near = jnp.where(grp == q, roll(part, E * q - 96), t_near)

    kz_own = jnp.where(up, E - 1 - lane32, lane32)
    kz_near = jnp.where(up, lane32, E - 1 - lane32)
    alpha_z = [corners(near_r[2][at : at + 1])[0] for at in (3, 2)]
    planes, outer = [], []
    for which, at, kz, rows_ab, rows_h, wplane in (
        (0, 3, kz_own, own_ab, own_h, w_near),
        (1, 2, kz_near, near_ab, near_h, s_z),
    ):
        weights = jnp.where(sub8 == grp, column(near_r[2][at : at + 1], kz), 0.0)
        ca = dot(weights, rows_ab)
        ch = dot(weights, rows_h)
        first_row = jnp.zeros((1, N), F32)
        last_row = jnp.zeros((1, N), F32)
        for q in range(4):
            first_row = jnp.where(grp == q, roll(ca[q : q + 1], E * q), first_row)
            last_row = jnp.where(grp == q, roll(ca[q : q + 1], E * q - E), last_row)
        mark = jnp.concatenate(
            [
                jnp.where((sub8 == grp) & (lane32 == 0), 1.0, 0.0),
                jnp.where((sub8 == grp) & (lane32 == E - 1), 1.0, 0.0),
            ],
            1,
        )
        marked = dot_first(ch, mark)
        plane = marked[0:E, 0:N] + marked[E : 2 * E, N : 2 * N] + alpha_z[which] * wplane
        plane = plane + jnp.where(row32 == 0, first_row, 0.0)
        plane = plane + jnp.where(row32 == E - 1, last_row, 0.0)
        pl_ref[which] = plane
        cols = jnp.concatenate(
            [
                jnp.where(sub8 == grp, column(near_r[1][at : at + 1], lane32), 0.0),
                jnp.where(sub8 == grp, column(near_r[1][at : at + 1], E - 1 - lane32), 0.0),
            ],
            1,
        )
        sides = dot_first(ca, cols)
        outer.append(sides[64:96, 0:N] + sides[96:128, N : 2 * N])

    halo_low, halo_up = halo[0:E], halo[E : 2 * E]
    f_ref[0:E, :] = f_ref[0:E, :] + halo_low
    f_ref[(E - 1) * E : E * E, :] = f_ref[(E - 1) * E : E * E, :] + halo_up
    at = pl.ds(0, E, stride=E)
    f_ref[at, :] = f_ref[at, :] + ab[0:E]
    at = pl.ds(E - 1, E, stride=E)
    f_ref[at, :] = f_ref[at, :] + ab[E : 2 * E]

    def on_face(plane, j):
        first = roll(plane, N - j)
        last = roll(plane, lax.rem(N + E - 1 - j, N))
        return jnp.where(face_lane, jnp.where(up, last, first), 0.0)

    def z_halo(j, carry):
        at = pl.ds(pl.multiple_of(j * E, E), E)
        f_ref[at, :] = f_ref[at, :] + on_face(w_near, j)
        return carry

    lax.fori_loop(0, E, z_halo, 0)

    def last_rows(i):
        x = jnp.where(sub8 == 3, pl_ref[0, pl.ds(i, 1), :], 0.0)
        return jnp.where(sub8 == 2, pl_ref[1, pl.ds(i, 1), :], x)

    solve_i(last_rows)
    ends_z = []
    for which, at in ((0, 3), (1, 2)):
        blocks = inverse_blocks(near_r[1][at : at + 1])
        ends_z.append(dot(e_ref[:, at, :], blocks) + outer[which])
    sigma = ends_z[0] + t_own
    tau = ends_z[1] + t_near
    c_plane = -gz * (sigma - tau) / (1.0 + gz * (alpha_z[0] + alpha_z[1]))

    solve_j(ab[64:96], ab[96:128])
    zblocks = inverse_blocks(own[2])

    def finish(t, carry):
        outs = []
        for m in range(4):
            j = t * 4 + m
            at = pl.ds(pl.multiple_of(j * E, E), E)
            d2 = g_ref[at, :] + on_face(c_plane, j)
            outs.append(u_ref[at, :] + dot(d2, zblocks))
        outs = swap_blocks(outs, grp)
        cols = pl.ds(pl.multiple_of(t * N, N), N)
        for b in range(2):
            out_c[b, :, cols] = outs[2 * b]
            out_b[b, :, cols] = outs[2 * b + 1]
        return carry

    lax.fori_loop(0, 8, finish, 0)

    arrive.wait_send()

    def left1(count):
        part = send1.at[pl.ds(0, 8 * count)]
        pltpu.make_async_remote_copy(
            part, part, ss1, rs1, device_id=(me,), device_id_type=MESH
        ).wait_send()

    @pl.when(owner)
    def _():
        left1(OWNERS - 1)
        part = send2.at[pl.ds(0, 8 * (N - 1))]
        pltpu.make_async_remote_copy(
            part, part, ss2, rs2, device_id=(me,), device_id_type=MESH
        ).wait_send()

    @pl.when(jnp.logical_not(owner))
    def _():
        left1(OWNERS)


def body(calcium, buffer, fraction, rates, inverses, neighbors, ranks):
    vmem = pl.BlockSpec(memory_space=pltpu.VMEM)
    smem = pl.BlockSpec(memory_space=pltpu.SMEM)
    shape = jax.ShapeDtypeStruct(calcium.shape, F32)
    field = pltpu.VMEM((E * E, N), F32)
    return pl.pallas_call(
        step_kernel,
        out_shape=(shape, shape),
        in_specs=[smem, smem, vmem, vmem, vmem, vmem, vmem],
        out_specs=(vmem, vmem),
        scratch_shapes=[
            field,
            field,
            field,
            field,
            pltpu.VMEM((1, 1, N), F32),
            pltpu.VMEM((N, 1, N), F32),
            pltpu.VMEM((8 * OWNERS, N), F32),
            pltpu.VMEM((8 * N, N), F32),
            pltpu.VMEM((8 * N, N), F32),
            pltpu.VMEM((8 * OWNERS, N), F32),
            pltpu.VMEM((2, E, N), F32),
            pltpu.VMEM((2, E, N), F32),
            pltpu.VMEM((E, 8, N), F32),
            pltpu.VMEM((E, 8, N), F32),
            pltpu.VMEM((E, 8, N), F32),
            pltpu.VMEM((3, E, N), F32),
            pltpu.VMEM((4, 256, N), BF16),
            pltpu.VMEM((4, N, 256), BF16),
            pltpu.VMEM((19, 256, N), F32),
            pltpu.VMEM((11, 256, N), F32),
        ]
        + [pltpu.SemaphoreType.DMA] * 6
        + [pltpu.SemaphoreType.DMA((3,))],
        compiler_params=pltpu.CompilerParams(
            collective_id=0, has_side_effects=True, vmem_limit_bytes=60 * 1024 * 1024
        ),
    )(rates, neighbors, neighbors, ranks, calcium, buffer, fraction)


def solution(mesh):
    in_specs = (
        P("bricks", None, None),
        P("bricks", None, None),
        P("bricks", None, None),
        P("bricks", None, None),
        P("bricks", None, None, None, None),
        P(),
        P(),
    )
    out_specs = (P("bricks", None, None), P("bricks", None, None))
    return jax.shard_map(body, mesh=mesh, in_specs=in_specs, out_specs=out_specs, check_vma=False)
```

time: 668 us -> 62.1 us (0.09); the launches traced: 659 us -> 61.9 us
  local copies, waits for them, and re-layouts: 330 us -> 3.78 us
  other arithmetic: 115 us -> 0 us
  blocking collectives: 89.7 us -> 0 us
  Pallas kernels: 0 us -> 57.5 us
  starting transfers between devices: 51.4 us -> 0 us
  waiting for transfers between devices: 48.3 us -> 0 us
  matrix products: 16.1 us -> 0 us
  between operations: 7.91 us -> 0.65 us
    slice x566 -> x0, local copies, waits for them, and re-layouts: 124 us -> none  [the longest x147 31.8 us: sorted_solve(): lax.associative_scan(compose_affine, (-f0[:, :, None], e0), reverse=True,...]
    gather x63 -> x0, local copies, waits for them, and re-layouts: 89.2 us -> none  [the longest x18 35 us: chain_order(): pointer = jnp.take(pointer, pointer, axis=0)]
    all_gather x2 -> x0, blocking collectives: 71.8 us -> none  [the longest x1 38.2 us: body(): lax.all_gather(corners, 'bricks', axis=0, tiled=True)]
    pallas_call x0 -> x1, Pallas kernels: none -> 57.5 us  [body(): pl.pallas_call(step_kernel, out_shape=(shape, shape), in_specs=[smem, sme...]
    all_to_all x7 -> x0, starting transfers between devices: 51.4 us -> none  [the longest x2 19.2 us: solve(): lax.all_to_all(lined_jumps, 'bricks', split_axis=0, concat_axis=3, tiled=...]
    all_to_all x7 -> x0, waiting for transfers between devices: 48.3 us -> none  [the longest x2 25.6 us: solve(): lax.all_to_all(lined_jumps, 'bricks', split_axis=0, concat_axis=3, tiled=...]
    unnamed x551 -> x5, local copies, waits for them, and re-layouts: 40.1 us -> 3.78 us
    pad x228 -> x0, local copies, waits for them, and re-layouts: 32.2 us -> none  [the longest x144 14.5 us: sorted_solve(): summed = lax.associative_scan(compose_maps, maps, axis=0)]
  transfers between devices with their start and end apart: 7 -> 0, of which waited for: 6 -> 0; matrix products, arithmetic and copies ran while one was open for 36% -> 0% of each run, Pallas kernels for 0% -> 0%
where the time goes in v2:
time: 62.1 us; the launch traced here: 61.9 us
  Pallas kernels  57.5 us (93%)
  local copies, waits for them, and re-layouts  3.78 us (6%)
  between operations  0.65 us (1%)
    pallas_call x1, Pallas kernels, body(): pl.pallas_call(step_kernel, out_shape=(shape, shape), in_specs=[smem, sme...  57.5 us
    unnamed x5, local copies, waits for them, and re-layouts  3.78 us

profile of v2, /device:TPU:1, one launch (start us, length us, event | category | flops | bytes accessed | tf_op | source)
XLA Modules:
  0.0 61.9 jit_solution(12294319509281672342)
XLA Ops:
  0.6 1.4 %copy.8.rates = f32[2,3,2]{2,1,0:T(4,128)} copy(f32[2,3,2]{1,2,0:T(2,128)} %param.10) | data formatting | bytes 96 | tf_op args[3]
  2.0 57.5 %shard_map.77 = (f32[2,32,1024]{2,1,0:T(8,128)}, f32[2,32,1024]{2,1,0:T(8,128)}) custom-call(f32[2,3,2]{2,1,0:T(4,128)} %copy.8.rates, s32[3,2,256]{2,1,0:T(2,128)} %nbv.1, s32[3,2,256]{2,1,0:T(2,128)} %nbv.1, s32[3,256]{1,0:T(4,128)} %rkv.1, f32[2,32,1024]{2,1,0:T(8,128)} %cal.1, f32[2,32,1024]{2,1,0:T(8,128)} %buf.1, f32[2,32,1024]{2,1,0:T(8,128)} %frac.1), custom_call_target="tpu_custom_call" | custom-call | tf_op jit(solution)/shard_map/pallas_call | solution.py:771
  59.5 0.0 copy-start
  59.5 1.7 %copy.11 = f32[2,32,1024]{2,1,0:T(8,128)} copy(f32[2,32,1024]{2,1,0:T(8,128)} %get-tuple-element.4) | data formatting | bytes 524288
  61.2 0.0 copy-done
  61.2 0.7 %copy.12 = f32[2,32,1024]{2,1,0:T(8,128)} copy(f32[2,32,1024]{2,1,0:T(8,128)S(1)} %copy-done) | data formatting | bytes 524288
Async XLA Ops:
  59.5 1.7 %copy-start = (f32[2,32,1024]{2,1,0:T(8,128)S(1)}, f32[2,32,1024]{2,1,0:T(8,128)}, u32[]{:S(2)}) copy-start(f32[2,32,1024]{2,1,0:T(8,128)} %get-tuple-element.5) | copy-start | bytes 786436

commit v3 on v2

--- a/solution.py
+++ b/solution.py
@@ -124,14 +124,42 @@
     return out
 
 
+def split2(x):
+    a = x.astype(BF16)
+    return a, (x - a.astype(F32)).astype(BF16)
+
+
+def contract(a, b, dims):
+    ah, al = split2(a)
+    bh, bl = split2(b)
+    dims = (dims, ((), ()))
+    out = lax.dot_general(ah, bh, dims, preferred_element_type=F32)
+    out = out + lax.dot_general(al, bh, dims, preferred_element_type=F32)
+    return out + lax.dot_general(ah, bl, dims, preferred_element_type=F32)
+
+
 def dot(a, b):
-    return jnp.dot(a, b, precision=HIGH, preferred_element_type=F32)
+    return contract(a, b, ((1,), (0,)))
 
 
 def dot_first(a, b):
-    return lax.dot_general(
-        a, b, (((0,), (0,)), ((), ())), precision=HIGH, preferred_element_type=F32
+    return contract(a, b, ((0,), (0,)))
+
+
+def dot_last(a, b):
+    return contract(a, b, ((1,), (1,)))
+
+
+def packed_weights(w):
+    h, l = split2(w)
+    return jnp.concatenate(
+        [jnp.concatenate([h, l], 1), jnp.concatenate([h, jnp.zeros_like(h)], 1)], 0
     )
+
+
+def packed_dot(x, weights):
+    out = jnp.dot(jnp.concatenate(split2(x), 1), weights, preferred_element_type=F32)
+    return out[:, 0:N] + out[:, N : 2 * N]
 
 
 def one_hot(cond):
@@ -153,7 +181,7 @@
 
     def greet(step, carry):
         pl.semaphore_signal(
-            barrier, inc=1, device_id=(lax.rem(me + step, N),), device_id_type=MESH
+            barrier, inc=1, device_id=((me + step) & (N - 1),), device_id_type=MESH
         )
         return carry
 
@@ -169,7 +197,7 @@
     for d in range(3):
         r = jnp.zeros((1, N), F32)
         for q in range(4):
-            r = jnp.where(grp == q, rates[q // 2, d, q % 2], r)
+            r = jnp.where(grp == q, rates[q // 2, q % 2, d], r)
         own.append(r)
     message = jnp.where(lane32 == 0, own[0], jnp.where(lane32 == 1, own[1], own[2]))
     msg0[0] = message
@@ -203,17 +231,16 @@
 
     lax.fori_loop(0, 8, lay, 0)
 
-    m, e = sweep_terms(own[0], row32)
-    co0[0] = m
-    co0[1] = e
-    m, e = sweep_terms(own[1], row32)
-    co1[0] = m
-    co1[1] = e
+    for co, r in ((co0, own[0]), (co1, own[1])):
+        m, e = sweep_terms(r, row32)
+        co[0] = m
+        co[1] = e
+        co[2] = jnp.where(row32 == E - 1, 0.0, e)
 
     pl.semaphore_wait(barrier, N - 1)
 
     def send_rates(step, carry):
-        to = lax.rem(me + step, N)
+        to = (me + step) & (N - 1)
         pltpu.make_async_remote_copy(
             msg0, rt.at[pl.ds(me, 1)], ss0, rs0, device_id=(to,), device_id_type=MESH
         ).start()
@@ -231,7 +258,7 @@
 
     wz = lax.fori_loop(0, E, face, jnp.zeros((E, N), F32))
 
-    owner = lax.rem(me, 2) == 0
+    owner = (me & 1) == 0
 
     @pl.when(owner)
     def _():
@@ -271,6 +298,106 @@
             permt[b] = one_hot(lf == pos_b)
             permt[2 + b] = one_hot(lf == posz_b)
 
+    cu2 = jnp.where(lane32 < E - 1, 2.0 * own[2], 0.0)
+    cd2 = jnp.where(lane32 > 0, 2.0 * own[2], 0.0)
+    dg2 = cu2 + cd2
+    r1x2 = 2.0 * own[1]
+
+    def right_side(t, prev):
+        us = []
+        for m in range(5):
+            j = jnp.minimum(t * 4 + m, E - 1)
+            us.append(u_ref[pl.ds(pl.multiple_of(j * E, E), E), :])
+        for m in range(4):
+            j = t * 4 + m
+            at = pl.ds(pl.multiple_of(j * E, E), E)
+            u = us[m]
+            low = jnp.where(j == 0, 0.0, r1x2)
+            high = jnp.where(j == E - 1, 0.0, r1x2)
+            f_ref[at, :] = (
+                f_ref[at, :]
+                + cu2 * roll(u, -1)
+                + cd2 * roll(u, 1)
+                + low * prev
+                + high * us[m + 1]
+                - (dg2 + low + high) * u
+            )
+            prev = u
+        return prev
+
+    lax.fori_loop(0, E // 4, right_side, jnp.zeros((E, N), F32))
+
+    def solve_i(load_plane_row):
+        def forward(t, carry):
+            g, h = carry
+            for m in range(4):
+                i = t * 4 + m
+                at = pl.ds(i, E, stride=E)
+                g = co0[0, pl.ds(i, 1), :] * f_ref[at, :] + co0[1, pl.ds(i, 1), :] * g
+                t_ref[at, :] = g
+                if load_plane_row is not None:
+                    h = ecm[i] * load_plane_row(i) + ece[i] * h
+                    e_ref[i] = h
+            return g, h
+
+        lax.fori_loop(0, E // 4, forward, (jnp.zeros((E, N), F32), jnp.zeros((8, N), F32)))
+
+        def backward(t, carry):
+            x, h = carry
+            for m in range(4):
+                i = E - 1 - t * 4 - m
+                at = pl.ds(i, E, stride=E)
+                x = t_ref[at, :] + co0[2, pl.ds(i, 1), :] * x
+                t_ref[at, :] = x
+                if load_plane_row is not None:
+                    h = e_ref[i] + jnp.where(i == E - 1, 0.0, ece[i]) * h
+                    e_ref[i] = h
+            return x, h
+
+        lax.fori_loop(0, E // 4, backward, (jnp.zeros((E, N), F32), jnp.zeros((8, N), F32)))
+
+    def solve_j(extra_first, extra_last):
+        def forward(t, g):
+            for m in range(4):
+                j = t * 4 + m
+                at = pl.ds(pl.multiple_of(j * E, E), E)
+                d = t_ref[at, :] - 2.0 * u_ref[at, :]
+                if extra_first is not None and m == 0:
+                    d = d + jnp.where(j == 0, extra_first, 0.0)
+                if extra_last is not None and m == 3:
+                    d = d + jnp.where(j == E - 1, extra_last, 0.0)
+                g = co1[0, pl.ds(j, 1), :] * d + co1[1, pl.ds(j, 1), :] * g
+                g_ref[at, :] = g
+            return g
+
+        lax.fori_loop(0, E // 4, forward, jnp.zeros((E, N), F32))
+
+        def backward(t, x):
+            for m in range(4):
+                j = E - 1 - t * 4 - m
+                at = pl.ds(pl.multiple_of(j * E, E), E)
+                x = g_ref[at, :] + co1[2, pl.ds(j, 1), :] * x
+                g_ref[at, :] = x
+            return x
+
+        lax.fori_loop(0, E // 4, backward, jnp.zeros((E, N), F32))
+
+    solve_i(None)
+    solve_j(None, None)
+
+    rowN, colN = iota((N, N), 0), iota((N, N), 1)
+    kin = rowN & 31
+    weight = column(own[2], jnp.where(up, E - 1 - kin, kin))
+    weight = packed_weights(jnp.where((rowN >> 5) == (colN >> 5), weight, 0.0))
+
+    def face_mean(t, plane):
+        y = packed_dot(g_ref[pl.ds(pl.multiple_of(t * 8 * E, 8 * E), 8 * E), :], weight)
+        for m in range(8):
+            plane = jnp.where(lane32 == t * 8 + m, y[m * E : (m + 1) * E], plane)
+        return plane
+
+    t_own = lax.fori_loop(0, 4, face_mean, jnp.zeros((E, N), F32))
+
     keep.wait()
     arrive = pltpu.make_async_remote_copy(
         rt.at[pl.ds(0, N - 1)], rt.at[pl.ds(0, N - 1)], ss0, rs0, device_id=(me,), device_id_type=MESH
@@ -294,7 +421,7 @@
         got, there = rates_of(near[name])
         stack = jnp.where(sub8 == at, got, stack)
         has = jnp.where(sub8 == at, there, has)
-    stack = jnp.where(sub8 == 3, message, stack)
+    stack = jnp.where((sub8 >= 3) & (sub8 < 6), message, stack)
     near_r = []
     for d in range(3):
         x = roll(jnp.where(lane32 == d, stack, 0.0), -d)
@@ -305,148 +432,83 @@
     g2 = has * 2.0 * own[2] * near_r[2] / (own[2] + near_r[2])
     gyu, gyl, gz = g1[0:1], g1[1:2], g2[2:3]
 
-    cu2 = jnp.where(lane32 < E - 1, 2.0 * own[2], 0.0)
-    cd2 = jnp.where(lane32 > 0, 2.0 * own[2], 0.0)
-    dg2 = cu2 + cd2 + jnp.where(face_lane, 2.0 * gz, 0.0)
-    r1x2 = 2.0 * own[1]
-
-    def right_side(j, prev):
-        at = pl.ds(pl.multiple_of(j * E, E), E)
-        u = u_ref[at, :]
-        nxt = u_ref[pl.ds(pl.multiple_of(jnp.minimum(j + 1, E - 1) * E, E), E), :]
-        low = jnp.where(j == 0, 0.0, r1x2)
-        high = jnp.where(j == E - 1, 0.0, r1x2)
-        out_low = jnp.where(j == 0, 2.0 * gyl, r1x2)
-        out_high = jnp.where(j == E - 1, 2.0 * gyu, r1x2)
-        f_ref[at, :] = (
-            f_ref[at, :]
-            + cu2 * roll(u, -1)
-            + cd2 * roll(u, 1)
-            + low * prev
-            + high * nxt
-            - (dg2 + out_low + out_high) * u
-        )
-        return u
-
-    lax.fori_loop(0, E, right_side, jnp.zeros((E, N), F32))
-
     u_first, u_last = u_ref[0:E, :], u_ref[(E - 1) * E : E * E, :]
     s_up = 2.0 * gyu * u_last
     s_low = 2.0 * gyl * u_first
     s_z = 2.0 * gz * wz
-
     i8 = iota((E, 8, N), 0)
     mm, ee = sweep_terms(near_r[0][None], i8)
     ecm[...] = mm
     ece[...] = ee
-
-    def solve_i(load_plane_row):
-        def forward(i, carry):
-            g, h = carry
-            at = pl.ds(i, E, stride=E)
-            g = co0[0, pl.ds(i, 1), :] * f_ref[at, :] + co0[1, pl.ds(i, 1), :] * g
-            t_ref[at, :] = g
-            h = ecm[i] * load_plane_row(i) + ece[i] * h
-            e_ref[i] = h
-            return g, h
-
-        g, h = lax.fori_loop(0, E, forward, (jnp.zeros((E, N), F32), jnp.zeros((8, N), F32)))
-
-        def backward(step, carry):
-            i = E - 2 - step
-            x, h = carry
-            at = pl.ds(i, E, stride=E)
-            x = t_ref[at, :] + co0[1, pl.ds(i, 1), :] * x
-            t_ref[at, :] = x
-            h = e_ref[i] + ece[i] * h
-            e_ref[i] = h
-            return x, h
-
-        lax.fori_loop(0, E - 1, backward, (g, h))
-
-    def solve_j(extra_first, extra_last):
-        def forward(j, g):
-            at = pl.ds(pl.multiple_of(j * E, E), E)
-            d = t_ref[at, :] - 2.0 * u_ref[at, :]
-            if extra_first is not None:
-                d = d + jnp.where(j == 0, extra_first, 0.0) + jnp.where(j == E - 1, extra_last, 0.0)
-            g = co1[0, pl.ds(j, 1), :] * d + co1[1, pl.ds(j, 1), :] * g
-            g_ref[at, :] = g
-            return g
-
-        g = lax.fori_loop(0, E, forward, jnp.zeros((E, N), F32))
-
-        def backward(step, x):
-            j = E - 2 - step
-            at = pl.ds(pl.multiple_of(j * E, E), E)
-            x = g_ref[at, :] + co1[1, pl.ds(j, 1), :] * x
-            g_ref[at, :] = x
-            return x
-
-        lax.fori_loop(0, E - 1, backward, g)
-
     pl_ref[0] = s_up
     pl_ref[1] = s_low
     pl_ref[2] = s_z
 
-    def first_rows(i):
-        x = jnp.where(sub8 == 0, pl_ref[0, pl.ds(i, 1), :], 0.0)
-        x = jnp.where(sub8 == 1, pl_ref[1, pl.ds(i, 1), :], x)
-        return jnp.where(sub8 == 2, pl_ref[2, pl.ds(i, 1), :], x)
-
-    solve_i(first_rows)
-    for p in range(3):
-        pl_ref[p] = e_ref[:, p, :]
-    solve_j(None, None)
-
-    rowN, colN = iota((N, N), 0), iota((N, N), 1)
-    kin = rowN & 31
-    weight = column(own[2], jnp.where(up, E - 1 - kin, kin))
-    weight = jnp.where((rowN >> 5) == (colN >> 5), weight, 0.0)
-
-    def face_mean(j, plane):
-        y = g_ref[pl.ds(pl.multiple_of(j * E, E), E), :]
-        return jnp.where(lane32 == j, dot(y, weight), plane)
-
-    t_own = lax.fori_loop(0, E, face_mean, jnp.zeros((E, N), F32))
-
-    y0f = t_ref[pl.ds(0, E, stride=E), :]
-    y0l = t_ref[pl.ds(E - 1, E, stride=E), :]
-    y1f, y1l = g_ref[0:E, :], g_ref[(E - 1) * E : E * E, :]
+    h = jnp.zeros((8, N), F32)
+    for i in range(E):
+        x_up, x_low, x_z = [pl_ref[p, i : i + 1, :] for p in range(3)]
+        x = jnp.where(sub8 == 0, x_up, jnp.where(sub8 == 1, x_low, x_z))
+        x = jnp.where(sub8 == 3, -x_z, jnp.where(sub8 == 4, -x_low, jnp.where(sub8 == 5, -x_up, x)))
+        h = ecm[i] * x + ece[i] * h
+        e_ref[i] = h
+    for i in range(E - 2, -1, -1):
+        h = e_ref[i] + ece[i] * h
+        e_ref[i] = h
+    p_up, p_low, p_z, p_out, p_first, p_last = [e_ref[:, p, :] for p in range(6)]
+
+    alpha_1, eps_1 = corners(own[1])
+    out_first = jnp.where(row32 == 0, 1.0, 0.0)
+    out_last = jnp.where(row32 == E - 1, 1.0, 0.0)
+    y0f = t_ref[pl.ds(0, E, stride=E), :] + out_first * p_first[0:1] + out_last * p_last[0:1]
+    y0l = (
+        t_ref[pl.ds(E - 1, E, stride=E), :]
+        + out_first * p_first[E - 1 : E]
+        + out_last * p_last[E - 1 : E]
+    )
+    y1f = g_ref[0:E, :] + alpha_1 * p_first + eps_1 * p_last
+    y1l = g_ref[(E - 1) * E : E * E, :] + eps_1 * p_first + alpha_1 * p_last
     rows_a = jnp.transpose(jnp.concatenate([y0f, y0l, y1f, y1l], 0))
-    rows_b = jnp.transpose(jnp.concatenate([s_up, s_low, pl_ref[0], pl_ref[1]], 0))
-    pz = pl_ref[2]
-    v1z = column(near_r[1][2:3], lane32)
-    w1z = column(near_r[1][2:3], E - 1 - lane32)
-    ends = jnp.where(
-        (sub8 & 3) == grp, jnp.where(sub8 < 4, v1z, w1z), 0.0
-    )
-    ends_i = lax.dot_general(
-        ends, pz, (((1,), (1,)), ((), ())), precision=HIGH, preferred_element_type=F32
-    )
-    ends_i = jnp.concatenate([ends_i, jnp.zeros((8, N - E), F32)], 1)
+    rows_b = jnp.transpose(jnp.concatenate([s_up, s_low, p_up, p_low], 0))
+    group8 = (sub8 & 3) == grp
+    ends_i = []
+    for p, at in ((p_z, 2), (p_out, 3)):
+        r1 = near_r[1][at : at + 1]
+        ends = jnp.where(sub8 < 4, column(r1, lane32), column(r1, E - 1 - lane32))
+        x = dot_last(jnp.where(group8, ends, 0.0), p)
+        ends_i.append(jnp.concatenate([x, jnp.zeros((8, N - E), F32)], 1))
+
+    def end_row(p, x, q):
+        c = jnp.where(lane < 32, roll(p[0:1], -E * q), roll(p[E - 1 : E], E - E * q))
+        c = jnp.where(lane < 64, c, roll(x[q : q + 1], 64))
+        return jnp.where(lane < 96, c, roll(x[q + 4 : q + 5], 96))
+
     for q in range(4):
         b, sp = q // 2, q % 2
         base = sp * 8 + b * 4
-        send1[pl.ds(base, E, stride=16), :] = rows_a[q * E : (q + 1) * E]
-        send1[pl.ds(base + 1, E, stride=16), :] = rows_b[q * E : (q + 1) * E]
-        c = jnp.where(lane < 32, roll(pz[0:1], -E * q), roll(pz[E - 1 : E], E - E * q))
-        c = jnp.where(lane < 64, c, roll(ends_i[q : q + 1], 64))
-        c = jnp.where(lane < 96, c, roll(ends_i[q + 4 : q + 5], 96))
-        kf = jnp.where(near["zu"][b] >= 0, 0, E - 1)
-        send1[pl.ds(base + 2, E, stride=16), :] = jnp.where(row32 == kf, c, 0.0)
-        dd = jnp.where(
-            lane < 32, roll(s_z, -E * q), jnp.where(lane < 64, roll(t_own, E - E * q), 0.0)
-        )
-        send1[pl.ds(base + 3, E, stride=16), :] = roll(dd, 64)
+        mine_up = near["zu"][b] >= 0
+        kf = jnp.where(mine_up, E - 1, 0)
+        kn = jnp.where(mine_up, 0, E - 1)
+        part_a, part_b = rows_a[q * E : (q + 1) * E], rows_b[q * E : (q + 1) * E]
+        send1[pl.ds(base, E, stride=16), :] = part_a + jnp.where(
+            row32 == kf, end_row(p_out, ends_i[1], q), 0.0
+        )
+        send1[pl.ds(base + 1, E, stride=16), :] = part_b
+        send1[pl.ds(base + 2, E, stride=16), :] = jnp.where(
+            row32 == kn, end_row(p_z, ends_i[0], q), 0.0
+        )
+        out = jnp.where(lane < 32, -roll(part_b, -E), -roll(part_b, E))
+        zt = jnp.where(lane < 96, roll(s_z, 64 - E * q), roll(t_own, 96 - E * q))
+        send1[pl.ds(base + 3, E, stride=16), :] = jnp.where(lane < 64, out, zt)
+
+    mine = me >> 1
 
     def block(ref, index):
         return ref.at[pl.ds(pl.multiple_of(index * 8, 8), 8)]
 
-    mine = me // 2
+    mine = me >> 1
 
     def send_ends(step, carry):
-        o = lax.rem(mine + step, OWNERS)
+        o = (mine + step) & (OWNERS - 1)
         pltpu.make_async_remote_copy(
             block(send1, o), block(land1, me), ss1, rs1, device_id=(2 * o,), device_id_type=MESH
         ).start()
@@ -464,7 +526,7 @@
     def _():
         local = pltpu.make_async_copy(block(send1, mine), block(land1, me), own_sem.at[1])
         local.start()
-        sp32 = lax.rem(mine, 2) * 32
+        sp32 = (mine & 1) * 32
         table = rt[:, 0, :]
         ordered = pick(perm[0], table) + pick(perm[1], roll(table, 64))
         pick_at = iota((N, 2 * N), 0)
@@ -550,7 +612,7 @@
         yd = ordered_rows(3, 0)
         bl = kk[0] * roll(yb, 1, 0)
         bu = link_next * roll(yb, -1, 0)
-        out2 = jnp.where(lane < 32, bl, jnp.where(lane < 64, bu, yd))
+        out2 = jnp.where(lane < 32, bl, jnp.where(lane < 64, bu, 0.0)) + yd
         straight = jnp.where(lane < 96, bl, bu)
         crossed = jnp.where(lane < 96, roll(bu, -32), roll(bl, 32))
         ya = ya + jnp.where(lane >= 64, chain[4] * straight + chain[5] * crossed, 0.0)
@@ -612,7 +674,7 @@
                 send2[pl.ds(b * 4 + kind, N, stride=8), :] = pick(permt[which], what)
 
         def send_back(step, carry):
-            to = lax.rem(me + step, N)
+            to = (me + step) & (N - 1)
             pltpu.make_async_remote_copy(
                 block(send2, to), block(land2, mine), ss2, rs2, device_id=(to,), device_id_type=MESH
             ).start()
@@ -654,11 +716,12 @@
 
     kz_own = jnp.where(up, E - 1 - lane32, lane32)
     kz_near = jnp.where(up, lane32, E - 1 - lane32)
+    delta_z = w_near - s_z
     alpha_z = [corners(near_r[2][at : at + 1])[0] for at in (3, 2)]
     planes, outer = [], []
     for which, at, kz, rows_ab, rows_h, wplane in (
-        (0, 3, kz_own, own_ab, own_h, w_near),
-        (1, 2, kz_near, near_ab, near_h, s_z),
+        (0, 3, kz_own, own_ab, own_h, delta_z),
+        (1, 2, kz_near, near_ab, near_h, -delta_z),
     ):
         weights = jnp.where(sub8 == grp, column(near_r[2][at : at + 1], kz), 0.0)
         ca = dot(weights, rows_ab)
@@ -700,15 +763,17 @@
 
     def on_face(plane, j):
         first = roll(plane, N - j)
-        last = roll(plane, lax.rem(N + E - 1 - j, N))
+        last = roll(plane, (N + E - 1 - j) & (N - 1))
         return jnp.where(face_lane, jnp.where(up, last, first), 0.0)
 
-    def z_halo(j, carry):
-        at = pl.ds(pl.multiple_of(j * E, E), E)
-        f_ref[at, :] = f_ref[at, :] + on_face(w_near, j)
+    def z_halo(t, carry):
+        for m in range(4):
+            j = t * 4 + m
+            at = pl.ds(pl.multiple_of(j * E, E), E)
+            f_ref[at, :] = f_ref[at, :] + on_face(delta_z, j)
         return carry
 
-    lax.fori_loop(0, E, z_halo, 0)
+    lax.fori_loop(0, E // 4, z_halo, 0)
 
     def last_rows(i):
         x = jnp.where(sub8 == 3, pl_ref[0, pl.ds(i, 1), :], 0.0)
@@ -724,23 +789,26 @@
     c_plane = -gz * (sigma - tau) / (1.0 + gz * (alpha_z[0] + alpha_z[1]))
 
     solve_j(ab[64:96], ab[96:128])
-    zblocks = inverse_blocks(own[2])
+    zblocks = packed_weights(inverse_blocks(own[2]))
 
     def finish(t, carry):
-        outs = []
-        for m in range(4):
-            j = t * 4 + m
-            at = pl.ds(pl.multiple_of(j * E, E), E)
-            d2 = g_ref[at, :] + on_face(c_plane, j)
-            outs.append(u_ref[at, :] + dot(d2, zblocks))
-        outs = swap_blocks(outs, grp)
-        cols = pl.ds(pl.multiple_of(t * N, N), N)
-        for b in range(2):
-            out_c[b, :, cols] = outs[2 * b]
-            out_b[b, :, cols] = outs[2 * b + 1]
+        d2 = []
+        for m in range(8):
+            at = pl.ds(pl.multiple_of((t * 8 + m) * E, E), E)
+            d2.append(g_ref[at, :] + on_face(c_plane, t * 8 + m))
+        d3 = packed_dot(jnp.concatenate(d2, 0), zblocks)
+        d3 = d3 + u_ref[pl.ds(pl.multiple_of(t * 8 * E, 8 * E), 8 * E), :]
+        for half in range(2):
+            outs = swap_blocks(
+                [d3[(half * 4 + m) * E : (half * 4 + m + 1) * E] for m in range(4)], grp
+            )
+            cols = pl.ds(pl.multiple_of((t * 2 + half) * N, N), N)
+            for b in range(2):
+                out_c[b, :, cols] = outs[2 * b]
+                out_b[b, :, cols] = outs[2 * b + 1]
         return carry
 
-    lax.fori_loop(0, 8, finish, 0)
+    lax.fori_loop(0, 4, finish, 0)
 
     arrive.wait_send()
 
@@ -784,8 +852,8 @@
             pltpu.VMEM((8 * N, N), F32),
             pltpu.VMEM((8 * N, N), F32),
             pltpu.VMEM((8 * OWNERS, N), F32),
-            pltpu.VMEM((2, E, N), F32),
-            pltpu.VMEM((2, E, N), F32),
+            pltpu.VMEM((3, E, N), F32),
+            pltpu.VMEM((3, E, N), F32),
             pltpu.VMEM((E, 8, N), F32),
             pltpu.VMEM((E, 8, N), F32),
             pltpu.VMEM((E, 8, N), F32),
@@ -800,7 +868,7 @@
         compiler_params=pltpu.CompilerParams(
             collective_id=0, has_side_effects=True, vmem_limit_bytes=60 * 1024 * 1024
         ),
-    )(rates, neighbors, neighbors, ranks, calcium, buffer, fraction)
+    )(jnp.transpose(rates, (0, 2, 1)), neighbors, neighbors, ranks, calcium, buffer, fraction)
 
 
 def solution(mesh):

time: 62.1 us -> 47.4 us (0.76)
  Pallas kernels: 57.5 us -> 44.1 us
  local copies, waits for them, and re-layouts: 3.78 us -> 2.42 us
    pallas_call x1, Pallas kernels: 57.5 us -> 44.1 us  [body(): pl.pallas_call(step_kernel, out_shape=(shape, shape), in_specs=[smem, sme...]
    unnamed x5 -> x4, local copies, waits for them, and re-layouts: 3.78 us -> 2.42 us
where the time goes in v3:
time: 47.4 us; the launch traced here: 47.2 us
  Pallas kernels  44.1 us (93%)
  local copies, waits for them, and re-layouts  2.42 us (5%)
  between operations  0.65 us (1%)
    pallas_call x1, Pallas kernels, body(): pl.pallas_call(step_kernel, out_shape=(shape, shape), in_specs=[smem, sme...  44.1 us
    unnamed x4, local copies, waits for them, and re-layouts  2.42 us

profile of v3, /device:TPU:1, one launch (start us, length us, event | category | flops | bytes accessed | tf_op | source)
XLA Modules:
  0.0 47.2 jit_solution(12715515798447320466)
XLA Ops:
  0.6 44.1 %shard_map.77 = (f32[2,32,1024]{2,1,0:T(8,128)}, f32[2,32,1024]{2,1,0:T(8,128)}) custom-call(f32[2,2,3]{2,1,0:T(2,128)} %bitcast.1, s32[3,2,256]{2,1,0:T(2,128)} %nbv.1, s32[3,2,256]{2,1,0:T(2,128)} %nbv.1, s32[3,256]{1,0:T(4,128)} %rkv.1, f32[2,32,1024]{2,1,0:T(8,128)} %cal.1, f32[2,32,1024]{2,1,0:T(8,128)} %buf.1, f32[2,32,1024]{2,1,0:T(8,128)} %frac.1), custom_call_target="tpu_custom_call" | custom-call | tf_op jit(solution)/shard_map/pallas_call | solution.py:839
  44.8 0.0 copy-start
  44.8 1.7 %copy.10 = f32[2,32,1024]{2,1,0:T(8,128)} copy(f32[2,32,1024]{2,1,0:T(8,128)} %get-tuple-element.4) | data formatting | bytes 524288
  46.5 0.0 copy-done
  46.5 0.7 %copy.11 = f32[2,32,1024]{2,1,0:T(8,128)} copy(f32[2,32,1024]{2,1,0:T(8,128)S(1)} %copy-done) | data formatting | bytes 524288
Async XLA Ops:
  44.8 1.7 %copy-start = (f32[2,32,1024]{2,1,0:T(8,128)S(1)}, f32[2,32,1024]{2,1,0:T(8,128)}, u32[]{:S(2)}) copy-start(f32[2,32,1024]{2,1,0:T(8,128)} %get-tuple-element.5) | copy-start | bytes 786436

commit v4 on v3

--- a/solution.py
+++ b/solution.py
@@ -172,20 +172,17 @@
 
 def step_kernel(
     rates, nbs, nbv, rkv, cal, buf, frac, out_c, out_b,
-    u_ref, f_ref, t_ref, g_ref, msg0, rt, send1, land1, send2, land2,
+    u_ref, f_ref, t_ref, g_ref, rt, send1, land1, send2, land2,
     co0, co1, ecm, ece, e_ref, pl_ref, perm, permt, kk, chain,
     ss0, rs0, ss1, rs1, ss2, rs2, own_sem,
 ):
     me = lax.axis_index("bricks")
     barrier = pltpu.get_barrier_semaphore()
 
-    def greet(step, carry):
-        pl.semaphore_signal(
-            barrier, inc=1, device_id=((me + step) & (N - 1),), device_id_type=MESH
-        )
-        return carry
-
-    lax.fori_loop(1, N, greet, 0)
+    stages = [(1, [me ^ t for t in range(1, 8)]), (8, [me ^ (8 * t) for t in range(1, 16)])]
+    greeted = [to for _, group in stages for to in group]
+    for to in greeted:
+        pl.semaphore_signal(barrier, inc=1, device_id=(to,), device_id_type=MESH)
 
     lane = iota((1, N), 1)
     lane32 = lane & 31
@@ -200,7 +197,7 @@
             r = jnp.where(grp == q, rates[q // 2, q % 2, d], r)
         own.append(r)
     message = jnp.where(lane32 == 0, own[0], jnp.where(lane32 == 1, own[1], own[2]))
-    msg0[0] = message
+    rt[me] = message
     near = {}
     for name, d, side in (("yl", 1, 0), ("yu", 1, 1), ("zl", 2, 0), ("zu", 2, 1)):
         near[name] = [nbs[d, side, 2 * me + b] for b in range(2)]
@@ -237,18 +234,27 @@
         co[1] = e
         co[2] = jnp.where(row32 == E - 1, 0.0, e)
 
-    pl.semaphore_wait(barrier, N - 1)
-
-    def send_rates(step, carry):
-        to = (me + step) & (N - 1)
-        pltpu.make_async_remote_copy(
-            msg0, rt.at[pl.ds(me, 1)], ss0, rs0, device_id=(to,), device_id_type=MESH
-        ).start()
-        return carry
-
-    lax.fori_loop(1, N, send_rates, 0)
-    keep = pltpu.make_async_copy(msg0, rt.at[pl.ds(me, 1)], own_sem.at[0])
-    keep.start()
+    pl.semaphore_wait(barrier, len(greeted))
+
+    def rates_block(unit):
+        return rt.at[pl.ds(me & (N - unit), unit)]
+
+    def gather_start(at):
+        unit, group = stages[at]
+        for to in group:
+            pltpu.make_async_remote_copy(
+                rates_block(unit), rates_block(unit), ss0.at[at], rs0.at[at],
+                device_id=(to,), device_id_type=MESH,
+            ).start()
+
+    def gather_all(at):
+        unit, group = stages[at]
+        part = rt.at[pl.ds(0, unit * len(group))]
+        return pltpu.make_async_remote_copy(
+            part, part, ss0.at[at], rs0.at[at], device_id=(me,), device_id_type=MESH
+        )
+
+    gather_start(0)
 
     def face(j, plane):
         u = u_ref[pl.ds(pl.multiple_of(j * E, E), E), :]
@@ -257,6 +263,9 @@
         return jnp.where(lane32 == j, jnp.where(up, last, first), plane)
 
     wz = lax.fori_loop(0, E, face, jnp.zeros((E, N), F32))
+
+    gather_all(0).wait_recv()
+    gather_start(1)
 
     owner = (me & 1) == 0
 
@@ -398,11 +407,7 @@
 
     t_own = lax.fori_loop(0, 4, face_mean, jnp.zeros((E, N), F32))
 
-    keep.wait()
-    arrive = pltpu.make_async_remote_copy(
-        rt.at[pl.ds(0, N - 1)], rt.at[pl.ds(0, N - 1)], ss0, rs0, device_id=(me,), device_id_type=MESH
-    )
-    arrive.wait_recv()
+    gather_all(1).wait_recv()
 
     def rates_of(indices):
         rows = []
@@ -524,7 +529,7 @@
 
     @pl.when(owner)
     def _():
-        local = pltpu.make_async_copy(block(send1, mine), block(land1, me), own_sem.at[1])
+        local = pltpu.make_async_copy(block(send1, mine), block(land1, me), own_sem.at[0])
         local.start()
         sp32 = (mine & 1) * 32
         table = rt[:, 0, :]
@@ -681,7 +686,7 @@
             return carry
 
         lax.fori_loop(1, N, send_back, 0)
-        local = pltpu.make_async_copy(block(send2, me), block(land2, mine), own_sem.at[2])
+        local = pltpu.make_async_copy(block(send2, me), block(land2, mine), own_sem.at[1])
         local.start()
         local.wait()
 
@@ -810,7 +815,8 @@
 
     lax.fori_loop(0, 4, finish, 0)
 
-    arrive.wait_send()
+    for at in range(2):
+        gather_all(at).wait_send()
 
     def left1(count):
         part = send1.at[pl.ds(0, 8 * count)]
@@ -846,7 +852,6 @@
             field,
             field,
             field,
-            pltpu.VMEM((1, 1, N), F32),
             pltpu.VMEM((N, 1, N), F32),
             pltpu.VMEM((8 * OWNERS, N), F32),
             pltpu.VMEM((8 * N, N), F32),
@@ -863,8 +868,9 @@
             pltpu.VMEM((19, 256, N), F32),
             pltpu.VMEM((11, 256, N), F32),
         ]
-        + [pltpu.SemaphoreType.DMA] * 6
-        + [pltpu.SemaphoreType.DMA((3,))],
+        + [pltpu.SemaphoreType.DMA((2,))] * 2
+        + [pltpu.SemaphoreType.DMA] * 4
+        + [pltpu.SemaphoreType.DMA((2,))],
         compiler_params=pltpu.CompilerParams(
             collective_id=0, has_side_effects=True, vmem_limit_bytes=60 * 1024 * 1024
         ),

time: 47.4 us -> 45.4 us (0.958)
  Pallas kernels: 44.1 us -> 42.2 us
    pallas_call x1, Pallas kernels: 44.1 us -> 42.2 us  [body(): pl.pallas_call(step_kernel, out_shape=(shape, shape), in_specs=[smem, sme...]
where the time goes in v4:
time: 45.4 us; the launch traced here: 45.3 us
  Pallas kernels  42.2 us (93%)
  local copies, waits for them, and re-layouts  2.42 us (5%)
  between operations  0.65 us (1%)
    pallas_call x1, Pallas kernels, body(): pl.pallas_call(step_kernel, out_shape=(shape, shape), in_specs=[smem, sme...  42.2 us
    unnamed x4, local copies, waits for them, and re-layouts  2.42 us

profile of v4, /device:TPU:1, one launch (start us, length us, event | category | flops | bytes accessed | tf_op | source)
XLA Modules:
  0.0 45.3 jit_solution(9746502467719710354)
XLA Ops:
  0.6 42.2 %shard_map.77 = (f32[2,32,1024]{2,1,0:T(8,128)}, f32[2,32,1024]{2,1,0:T(8,128)}) custom-call(f32[2,2,3]{2,1,0:T(2,128)} %bitcast.1, s32[3,2,256]{2,1,0:T(2,128)} %nbv.1, s32[3,2,256]{2,1,0:T(2,128)} %nbv.1, s32[3,256]{1,0:T(4,128)} %rkv.1, f32[2,32,1024]{2,1,0:T(8,128)} %cal.1, f32[2,32,1024]{2,1,0:T(8,128)} %buf.1, f32[2,32,1024]{2,1,0:T(8,128)} %frac.1), custom_call_target="tpu_custom_call" | custom-call | tf_op jit(solution)/shard_map/pallas_call | solution.py:845
  42.9 0.0 copy-start
  42.9 1.7 %copy.10 = f32[2,32,1024]{2,1,0:T(8,128)} copy(f32[2,32,1024]{2,1,0:T(8,128)} %get-tuple-element.4) | data formatting | bytes 524288
  44.6 0.0 copy-done
  44.6 0.7 %copy.11 = f32[2,32,1024]{2,1,0:T(8,128)} copy(f32[2,32,1024]{2,1,0:T(8,128)S(1)} %copy-done) | data formatting | bytes 524288
Async XLA Ops:
  42.9 1.7 %copy-start = (f32[2,32,1024]{2,1,0:T(8,128)S(1)}, f32[2,32,1024]{2,1,0:T(8,128)}, u32[]{:S(2)}) copy-start(f32[2,32,1024]{2,1,0:T(8,128)} %get-tuple-element.5) | copy-start | bytes 786436

commit v5 on v4

--- a/solution.py
+++ b/solution.py
@@ -172,9 +172,10 @@
 
 def step_kernel(
     rates, nbs, nbv, rkv, cal, buf, frac, out_c, out_b,
-    u_ref, f_ref, t_ref, g_ref, rt, send1, land1, send2, land2,
-    co0, co1, ecm, ece, e_ref, pl_ref, perm, permt, kk, chain,
-    ss0, rs0, ss1, rs1, ss2, rs2, own_sem,
+    u_ref, f_ref, t_ref, g_ref, rt, send1b, land1b, send1c, land1c,
+    send2a, land2a, send2b, land2b, blocks_1,
+    co0, co1, ecm, ece, e_ref, pl_ref, ab_ref, perm, permt, kk, chain,
+    ss0, rs0, ss1b, rs1b, ss1c, rs1c, ss2a, rs2a, ss2b, rs2b, own_sem,
 ):
     me = lax.axis_index("bricks")
     barrier = pltpu.get_barrier_semaphore()
@@ -266,6 +267,205 @@
 
     gather_all(0).wait_recv()
     gather_start(1)
+
+    cu2 = jnp.where(lane32 < E - 1, 2.0 * own[2], 0.0)
+    cd2 = jnp.where(lane32 > 0, 2.0 * own[2], 0.0)
+    dg2 = cu2 + cd2
+    r1x2 = 2.0 * own[1]
+
+    def right_side(t, prev):
+        us = []
+        for m in range(5):
+            j = jnp.minimum(t * 4 + m, E - 1)
+            us.append(u_ref[pl.ds(pl.multiple_of(j * E, E), E), :])
+        for m in range(4):
+            j = t * 4 + m
+            at = pl.ds(pl.multiple_of(j * E, E), E)
+            u = us[m]
+            low = jnp.where(j == 0, 0.0, r1x2)
+            high = jnp.where(j == E - 1, 0.0, r1x2)
+            f_ref[at, :] = (
+                f_ref[at, :]
+                + cu2 * roll(u, -1)
+                + cd2 * roll(u, 1)
+                + low * prev
+                + high * us[m + 1]
+                - (dg2 + low + high) * u
+            )
+            prev = u
+        return prev
+
+    lax.fori_loop(0, E // 4, right_side, jnp.zeros((E, N), F32))
+
+    def solve_i(load_plane_row):
+        def forward(t, carry):
+            g, h = carry
+            for m in range(4):
+                i = t * 4 + m
+                at = pl.ds(i, E, stride=E)
+                g = co0[0, pl.ds(i, 1), :] * f_ref[at, :] + co0[1, pl.ds(i, 1), :] * g
+                t_ref[at, :] = g
+                if load_plane_row is not None:
+                    h = ecm[i] * load_plane_row(i) + ece[i] * h
+                    e_ref[i] = h
+            return g, h
+
+        lax.fori_loop(0, E // 4, forward, (jnp.zeros((E, N), F32), jnp.zeros((8, N), F32)))
+
+        def backward(t, carry):
+            x, h = carry
+            for m in range(4):
+                i = E - 1 - t * 4 - m
+                at = pl.ds(i, E, stride=E)
+                x = t_ref[at, :] + co0[2, pl.ds(i, 1), :] * x
+                t_ref[at, :] = x
+                if load_plane_row is not None:
+                    h = e_ref[i] + jnp.where(i == E - 1, 0.0, ece[i]) * h
+                    e_ref[i] = h
+            return x, h
+
+        lax.fori_loop(0, E // 4, backward, (jnp.zeros((E, N), F32), jnp.zeros((8, N), F32)))
+
+    def solve_j(extra, extra_first, extra_last):
+        def forward(t, g):
+            for m in range(4):
+                j = t * 4 + m
+                at = pl.ds(pl.multiple_of(j * E, E), E)
+                d = t_ref[at, :] - 2.0 * u_ref[at, :]
+                if extra is not None:
+                    d = d + extra(j)
+                if extra_first is not None and m == 0:
+                    d = d + jnp.where(j == 0, extra_first, 0.0)
+                if extra_last is not None and m == 3:
+                    d = d + jnp.where(j == E - 1, extra_last, 0.0)
+                g = co1[0, pl.ds(j, 1), :] * d + co1[1, pl.ds(j, 1), :] * g
+                g_ref[at, :] = g
+            return g
+
+        lax.fori_loop(0, E // 4, forward, jnp.zeros((E, N), F32))
+
+        def backward(t, x):
+            for m in range(4):
+                j = E - 1 - t * 4 - m
+                at = pl.ds(pl.multiple_of(j * E, E), E)
+                x = g_ref[at, :] + co1[2, pl.ds(j, 1), :] * x
+                g_ref[at, :] = x
+            return x
+
+        lax.fori_loop(0, E // 4, backward, jnp.zeros((E, N), F32))
+
+    solve_i(None)
+    solve_j(None, None, None)
+
+    rowN, colN = iota((N, N), 0), iota((N, N), 1)
+    kin = rowN & 31
+    weight = column(own[2], jnp.where(up, E - 1 - kin, kin))
+    weight = packed_weights(jnp.where((rowN >> 5) == (colN >> 5), weight, 0.0))
+
+    def face_mean(t, plane):
+        y = packed_dot(g_ref[pl.ds(pl.multiple_of(t * 8 * E, 8 * E), 8 * E), :], weight)
+        for m in range(8):
+            plane = jnp.where(lane32 == t * 8 + m, y[m * E : (m + 1) * E], plane)
+        return plane
+
+    t_own = lax.fori_loop(0, 4, face_mean, jnp.zeros((E, N), F32))
+
+    rows_a = jnp.transpose(
+        jnp.concatenate(
+            [
+                t_ref[pl.ds(0, E, stride=E), :],
+                t_ref[pl.ds(E - 1, E, stride=E), :],
+                g_ref[0:E, :],
+                g_ref[(E - 1) * E : E * E, :],
+            ],
+            0,
+        )
+    )
+    for q in range(4):
+        send1b[pl.ds(8 * (q % 2) + 3 * (q // 2), E, stride=16), :] = rows_a[q * E : (q + 1) * E]
+    mine = me >> 1
+
+    def block(ref, index, rows):
+        pitch = 8 if rows == 6 else rows
+        return ref.at[pl.ds(pl.multiple_of(index * pitch, pitch), rows)]
+
+    def to_owners(src, dst, rows, send_sem, recv_sem, local_sem):
+        def send(step, carry):
+            o = (mine + step) & (OWNERS - 1)
+            pltpu.make_async_remote_copy(
+                block(src, o, rows), block(dst, me, rows), send_sem, recv_sem,
+                device_id=(2 * o,), device_id_type=MESH,
+            ).start()
+            return carry
+
+        lax.fori_loop(1, OWNERS, send, 0)
+
+        @pl.when(jnp.logical_not(owner))
+        def _():
+            pltpu.make_async_remote_copy(
+                block(src, mine, rows), block(dst, me, rows), send_sem, recv_sem,
+                device_id=(2 * mine,), device_id_type=MESH,
+            ).start()
+
+        @pl.when(owner)
+        def _():
+            pltpu.make_async_copy(block(src, mine, rows), block(dst, me, rows), local_sem).start()
+
+    def to_owners_wait(src, rows, send_sem):
+        def left(count):
+            part = src.at[pl.ds(0, count * rows)]
+            pltpu.make_async_remote_copy(
+                part, part, send_sem, send_sem, device_id=(me,), device_id_type=MESH
+            ).wait_send()
+
+        @pl.when(owner)
+        def _():
+            left(OWNERS - 1)
+
+        @pl.when(jnp.logical_not(owner))
+        def _():
+            left(OWNERS)
+
+    def owner_wait(src, dst, rows, recv_sem, local_sem):
+        pltpu.make_async_copy(block(src, mine, rows), block(dst, me, rows), local_sem).wait()
+        part = dst.at[pl.ds(0, rows * (N - 1))]
+        pltpu.make_async_remote_copy(
+            part, part, recv_sem, recv_sem, device_id=(me,), device_id_type=MESH
+        ).wait_recv()
+
+    def to_bricks(src, dst, rows, send_sem, recv_sem, local_sem):
+        def send(step, carry):
+            to = (me + step) & (N - 1)
+            pltpu.make_async_remote_copy(
+                block(src, to, rows), block(dst, mine, rows), send_sem, recv_sem,
+                device_id=(to,), device_id_type=MESH,
+            ).start()
+            return carry
+
+        lax.fori_loop(1, N, send, 0)
+        pltpu.make_async_copy(block(src, me, rows), block(dst, mine, rows), local_sem).start()
+
+    def to_bricks_wait(src, rows, send_sem):
+        part = src.at[pl.ds(0, rows * (N - 1))]
+        pltpu.make_async_remote_copy(
+            part, part, send_sem, send_sem, device_id=(me,), device_id_type=MESH
+        ).wait_send()
+
+    def brick_wait(src, dst, rows, recv_sem, local_sem):
+        def arrived(count):
+            part = dst.at[pl.ds(0, count * rows)]
+            pltpu.make_async_remote_copy(
+                part, part, recv_sem, recv_sem, device_id=(me,), device_id_type=MESH
+            ).wait_recv()
+
+        @pl.when(owner)
+        def _():
+            pltpu.make_async_copy(block(src, me, rows), block(dst, mine, rows), local_sem).wait()
+            arrived(OWNERS - 1)
+
+        @pl.when(jnp.logical_not(owner))
+        def _():
+            arrived(OWNERS)
 
     owner = (me & 1) == 0
 
@@ -307,106 +507,6 @@
             permt[b] = one_hot(lf == pos_b)
             permt[2 + b] = one_hot(lf == posz_b)
 
-    cu2 = jnp.where(lane32 < E - 1, 2.0 * own[2], 0.0)
-    cd2 = jnp.where(lane32 > 0, 2.0 * own[2], 0.0)
-    dg2 = cu2 + cd2
-    r1x2 = 2.0 * own[1]
-
-    def right_side(t, prev):
-        us = []
-        for m in range(5):
-            j = jnp.minimum(t * 4 + m, E - 1)
-            us.append(u_ref[pl.ds(pl.multiple_of(j * E, E), E), :])
-        for m in range(4):
-            j = t * 4 + m
-            at = pl.ds(pl.multiple_of(j * E, E), E)
-            u = us[m]
-            low = jnp.where(j == 0, 0.0, r1x2)
-            high = jnp.where(j == E - 1, 0.0, r1x2)
-            f_ref[at, :] = (
-                f_ref[at, :]
-                + cu2 * roll(u, -1)
-                + cd2 * roll(u, 1)
-                + low * prev
-                + high * us[m + 1]
-                - (dg2 + low + high) * u
-            )
-            prev = u
-        return prev
-
-    lax.fori_loop(0, E // 4, right_side, jnp.zeros((E, N), F32))
-
-    def solve_i(load_plane_row):
-        def forward(t, carry):
-            g, h = carry
-            for m in range(4):
-                i = t * 4 + m
-                at = pl.ds(i, E, stride=E)
-                g = co0[0, pl.ds(i, 1), :] * f_ref[at, :] + co0[1, pl.ds(i, 1), :] * g
-                t_ref[at, :] = g
-                if load_plane_row is not None:
-                    h = ecm[i] * load_plane_row(i) + ece[i] * h
-                    e_ref[i] = h
-            return g, h
-
-        lax.fori_loop(0, E // 4, forward, (jnp.zeros((E, N), F32), jnp.zeros((8, N), F32)))
-
-        def backward(t, carry):
-            x, h = carry
-            for m in range(4):
-                i = E - 1 - t * 4 - m
-                at = pl.ds(i, E, stride=E)
-                x = t_ref[at, :] + co0[2, pl.ds(i, 1), :] * x
-                t_ref[at, :] = x
-                if load_plane_row is not None:
-                    h = e_ref[i] + jnp.where(i == E - 1, 0.0, ece[i]) * h
-                    e_ref[i] = h
-            return x, h
-
-        lax.fori_loop(0, E // 4, backward, (jnp.zeros((E, N), F32), jnp.zeros((8, N), F32)))
-
-    def solve_j(extra_first, extra_last):
-        def forward(t, g):
-            for m in range(4):
-                j = t * 4 + m
-                at = pl.ds(pl.multiple_of(j * E, E), E)
-                d = t_ref[at, :] - 2.0 * u_ref[at, :]
-                if extra_first is not None and m == 0:
-                    d = d + jnp.where(j == 0, extra_first, 0.0)
-                if extra_last is not None and m == 3:
-                    d = d + jnp.where(j == E - 1, extra_last, 0.0)
-                g = co1[0, pl.ds(j, 1), :] * d + co1[1, pl.ds(j, 1), :] * g
-                g_ref[at, :] = g
-            return g
-
-        lax.fori_loop(0, E // 4, forward, jnp.zeros((E, N), F32))
-
-        def backward(t, x):
-            for m in range(4):
-                j = E - 1 - t * 4 - m
-                at = pl.ds(pl.multiple_of(j * E, E), E)
-                x = g_ref[at, :] + co1[2, pl.ds(j, 1), :] * x
-                g_ref[at, :] = x
-            return x
-
-        lax.fori_loop(0, E // 4, backward, jnp.zeros((E, N), F32))
-
-    solve_i(None)
-    solve_j(None, None)
-
-    rowN, colN = iota((N, N), 0), iota((N, N), 1)
-    kin = rowN & 31
-    weight = column(own[2], jnp.where(up, E - 1 - kin, kin))
-    weight = packed_weights(jnp.where((rowN >> 5) == (colN >> 5), weight, 0.0))
-
-    def face_mean(t, plane):
-        y = packed_dot(g_ref[pl.ds(pl.multiple_of(t * 8 * E, 8 * E), 8 * E), :], weight)
-        for m in range(8):
-            plane = jnp.where(lane32 == t * 8 + m, y[m * E : (m + 1) * E], plane)
-        return plane
-
-    t_own = lax.fori_loop(0, 4, face_mean, jnp.zeros((E, N), F32))
-
     gather_all(1).wait_recv()
 
     def rates_of(indices):
@@ -426,7 +526,7 @@
         got, there = rates_of(near[name])
         stack = jnp.where(sub8 == at, got, stack)
         has = jnp.where(sub8 == at, there, has)
-    stack = jnp.where((sub8 >= 3) & (sub8 < 6), message, stack)
+    stack = jnp.where((sub8 >= 3) & (sub8 < 7), message, stack)
     near_r = []
     for d in range(3):
         x = roll(jnp.where(lane32 == d, stack, 0.0), -d)
@@ -461,19 +561,8 @@
         e_ref[i] = h
     p_up, p_low, p_z, p_out, p_first, p_last = [e_ref[:, p, :] for p in range(6)]
 
-    alpha_1, eps_1 = corners(own[1])
-    out_first = jnp.where(row32 == 0, 1.0, 0.0)
-    out_last = jnp.where(row32 == E - 1, 1.0, 0.0)
-    y0f = t_ref[pl.ds(0, E, stride=E), :] + out_first * p_first[0:1] + out_last * p_last[0:1]
-    y0l = (
-        t_ref[pl.ds(E - 1, E, stride=E), :]
-        + out_first * p_first[E - 1 : E]
-        + out_last * p_last[E - 1 : E]
-    )
-    y1f = g_ref[0:E, :] + alpha_1 * p_first + eps_1 * p_last
-    y1l = g_ref[(E - 1) * E : E * E, :] + eps_1 * p_first + alpha_1 * p_last
-    rows_a = jnp.transpose(jnp.concatenate([y0f, y0l, y1f, y1l], 0))
     rows_b = jnp.transpose(jnp.concatenate([s_up, s_low, p_up, p_low], 0))
+    rows_d = jnp.transpose(jnp.concatenate([p_first, p_last], 0))
     group8 = (sub8 & 3) == grp
     ends_i = []
     for p, at in ((p_z, 2), (p_out, 3)):
@@ -489,48 +578,38 @@
 
     for q in range(4):
         b, sp = q // 2, q % 2
-        base = sp * 8 + b * 4
         mine_up = near["zu"][b] >= 0
-        kf = jnp.where(mine_up, E - 1, 0)
-        kn = jnp.where(mine_up, 0, E - 1)
-        part_a, part_b = rows_a[q * E : (q + 1) * E], rows_b[q * E : (q + 1) * E]
-        send1[pl.ds(base, E, stride=16), :] = part_a + jnp.where(
-            row32 == kf, end_row(p_out, ends_i[1], q), 0.0
-        )
-        send1[pl.ds(base + 1, E, stride=16), :] = part_b
-        send1[pl.ds(base + 2, E, stride=16), :] = jnp.where(
-            row32 == kn, end_row(p_z, ends_i[0], q), 0.0
-        )
-        out = jnp.where(lane < 32, -roll(part_b, -E), -roll(part_b, E))
+        first_face = jnp.where(mine_up, 0.0, 1.0)
+        c_near, c_own = end_row(p_z, ends_i[0], q), end_row(p_out, ends_i[1], q)
+        send1c[4 * sp + 2 * b : 4 * sp + 2 * b + 1, :] = c_near * (1.0 - first_face)
+        send1c[4 * sp + 2 * b + 1 : 4 * sp + 2 * b + 2, :] = c_own * first_face
+        send1c[8 + 4 * sp + 2 * b : 8 + 4 * sp + 2 * b + 1, :] = c_near * first_face
+        send1c[8 + 4 * sp + 2 * b + 1 : 8 + 4 * sp + 2 * b + 2, :] = c_own * (1.0 - first_face)
+        send1b[pl.ds(8 * sp + 3 * b + 1, E, stride=16), :] = rows_b[q * E : (q + 1) * E]
         zt = jnp.where(lane < 96, roll(s_z, 64 - E * q), roll(t_own, 96 - E * q))
-        send1[pl.ds(base + 3, E, stride=16), :] = jnp.where(lane < 64, out, zt)
-
-    mine = me >> 1
-
-    def block(ref, index):
-        return ref.at[pl.ds(pl.multiple_of(index * 8, 8), 8)]
-
-    mine = me >> 1
-
-    def send_ends(step, carry):
-        o = (mine + step) & (OWNERS - 1)
-        pltpu.make_async_remote_copy(
-            block(send1, o), block(land1, me), ss1, rs1, device_id=(2 * o,), device_id_type=MESH
-        ).start()
-        return carry
-
-    lax.fori_loop(1, OWNERS, send_ends, 0)
-
-    @pl.when(jnp.logical_not(owner))
-    def _():
-        pltpu.make_async_remote_copy(
-            block(send1, mine), block(land1, me), ss1, rs1, device_id=(2 * mine,), device_id_type=MESH
-        ).start()
+        part = jnp.concatenate([rows_d[q * E : (q + 1) * E], jnp.zeros((E, 64), F32)], 1)
+        send1b[pl.ds(8 * sp + 3 * b + 2, E, stride=16), :] = jnp.where(lane < 64, part, zt)
+
+    to_owners(send1b, land1b, 6, ss1b, rs1b, own_sem.at[1])
+
+    face_owners = [0, 1, OWNERS - 2, OWNERS - 1]
+    for c, o in enumerate(face_owners):
+
+        @pl.when(me != 2 * o)
+        def _(c=c, o=o):
+            pltpu.make_async_remote_copy(
+                block(send1c, c, 4), block(land1c, me, 4), ss1c, rs1c,
+                device_id=(2 * o,), device_id_type=MESH,
+            ).start()
+
+        @pl.when(me == 2 * o)
+        def _(c=c):
+            pltpu.make_async_copy(block(send1c, c, 4), block(land1c, me, 4), own_sem.at[2]).start()
+
+    at_face = jnp.logical_and(owner, jnp.logical_or(mine < 2, mine >= OWNERS - 2))
 
     @pl.when(owner)
     def _():
-        local = pltpu.make_async_copy(block(send1, mine), block(land1, me), own_sem.at[0])
-        local.start()
         sp32 = (mine & 1) * 32
         table = rt[:, 0, :]
         ordered = pick(perm[0], table) + pick(perm[1], roll(table, 64))
@@ -599,30 +678,47 @@
         chain[8] = column(r1, j_of)
         chain[9] = column(r0, both_l)
         chain[10] = column(r0, E - 1 - both_l)
-        local.wait()
-        got = pltpu.make_async_remote_copy(
-            land1.at[pl.ds(0, 8 * (N - 1))], land1.at[pl.ds(0, 8 * (N - 1))], ss1, rs1,
-            device_id=(me,), device_id_type=MESH,
+
+        def ordered_rows(land, row, which):
+            rows = land.shape[0] // N
+            second = 3 if rows == 8 else 2
+            return pick(perm[which], land[pl.ds(row, N, stride=rows), :]) + pick(
+                perm[which + 1], land[pl.ds(row + second, N, stride=rows), :]
+            )
+
+        kk[0] = linked
+        owner_wait(send1b, land1b, 6, rs1b, own_sem.at[1])
+        yb = ordered_rows(land1b, 1, 0)
+        yd = ordered_rows(land1b, 2, 0)
+        bl = linked * roll(yb, 1, 0)
+        bu = roll(linked, -1, 0) * roll(yb, -1, 0)
+        swap = jnp.where(lane < 32, roll(yb, -32), roll(yb, 32))
+        out2 = jnp.where(lane < 64, jnp.where(lane < 32, bl, bu) - swap, yd)
+        for b in range(2):
+            for kind, which in ((0, b), (1, 2 + b)):
+                send2a[pl.ds(2 * b + kind, N, stride=4), :] = pick(permt[which], out2)
+        to_bricks(send2a, land2a, 4, ss2a, rs2a, own_sem.at[3])
+        straight = jnp.where(lane < 96, bl, bu) + roll(yd, 64)
+        crossed = jnp.where(lane < 96, roll(straight, -32), roll(straight, 32))
+        ends0 = jnp.where(
+            (lane == 0) | (lane == 63),
+            roll(straight, 64),
+            jnp.where(lane == 32, roll(straight, 65), jnp.where(lane == 31, roll(straight, 63), 0.0)),
         )
-        got.wait_recv()
-
-        def ordered_rows(kind, which):
-            return pick(perm[which], land1[pl.ds(kind, N, stride=8), :]) + pick(
-                perm[which + 1], land1[pl.ds(4 + kind, N, stride=8), :]
-            )
-
-        link_next = roll(kk[0], -1, 0)
-        ya = ordered_rows(0, 0) + ordered_rows(2, 2)
-        yb = ordered_rows(1, 0)
-        yd = ordered_rows(3, 0)
-        bl = kk[0] * roll(yb, 1, 0)
-        bu = link_next * roll(yb, -1, 0)
-        out2 = jnp.where(lane < 32, bl, jnp.where(lane < 64, bu, 0.0)) + yd
-        straight = jnp.where(lane < 96, bl, bu)
-        crossed = jnp.where(lane < 96, roll(bu, -32), roll(bl, 32))
-        ya = ya + jnp.where(lane >= 64, chain[4] * straight + chain[5] * crossed, 0.0)
-        ya = ya + jnp.where(lane == 0, roll(bl, 64), 0.0) + jnp.where(lane == 32, roll(bl, 65), 0.0)
-        ya = ya + jnp.where(lane == 31, roll(bu, 63), 0.0) + jnp.where(lane == 63, roll(bu, 64), 0.0)
+        chain[11] = ordered_rows(land1b, 0, 0) + jnp.where(
+            lane >= 64, chain[4] * straight + chain[5] * crossed, ends0
+        )
+
+        @pl.when(at_face)
+        def _():
+            pltpu.make_async_copy(block(send1c, 0, 4), block(land1c, me, 4), own_sem.at[2]).wait()
+            part = land1c.at[pl.ds(0, 4 * (N - 1))]
+            pltpu.make_async_remote_copy(
+                part, part, rs1c, rs1c, device_id=(me,), device_id_type=MESH
+            ).wait_recv()
+            chain[11] = chain[11] + ordered_rows(land1c, 0, 2) + ordered_rows(land1c, 1, 0)
+
+        ya = chain[11]
 
         def before_x(v, n):
             return jnp.concatenate([jnp.zeros((8 * n, N), F32), v[0 : 256 - 8 * n]], 0)
@@ -675,42 +771,17 @@
             jnp.where(lane < 96, bl_c, roll(br_c, 32)),
         )
         for b in range(2):
-            for kind, which, what in ((0, b, out1), (1, b, out2), (2, 2 + b, out1), (3, 2 + b, out2)):
-                send2[pl.ds(b * 4 + kind, N, stride=8), :] = pick(permt[which], what)
-
-        def send_back(step, carry):
-            to = (me + step) & (N - 1)
-            pltpu.make_async_remote_copy(
-                block(send2, to), block(land2, mine), ss2, rs2, device_id=(to,), device_id_type=MESH
-            ).start()
-            return carry
-
-        lax.fori_loop(1, N, send_back, 0)
-        local = pltpu.make_async_copy(block(send2, me), block(land2, mine), own_sem.at[1])
-        local.start()
-        local.wait()
-
-    def arrived2(count):
-        part = land2.at[pl.ds(0, 8 * count)]
-        pltpu.make_async_remote_copy(
-            part, part, ss2, rs2, device_id=(me,), device_id_type=MESH
-        ).wait_recv()
-
-    @pl.when(owner)
-    def _():
-        arrived2(OWNERS - 1)
-
-    @pl.when(jnp.logical_not(owner))
-    def _():
-        arrived2(OWNERS)
-
-    def gathered(kind):
+            for kind, which in ((0, b), (1, 2 + b)):
+                send2b[pl.ds(2 * b + kind, N, stride=4), :] = pick(permt[which], out1)
+        to_bricks(send2b, land2b, 4, ss2b, rs2b, own_sem.at[4])
+
+    def gathered(land, kind):
         return jnp.concatenate(
-            [land2[pl.ds((q % 2) * 8 + (q // 2) * 4 + kind, E, stride=16), :] for q in range(4)], 0
+            [land[pl.ds(q % 2 * 4 + q // 2 * 2 + kind, E, stride=8), :] for q in range(4)], 0
         )
 
-    own_ab, own_h, near_ab, near_h = [gathered(kind) for kind in range(4)]
-    ab = jnp.transpose(own_ab)
+    brick_wait(send2a, land2a, 4, rs2a, own_sem.at[3])
+    own_h, near_h = gathered(land2a, 0), gathered(land2a, 1)
     halo = jnp.transpose(own_h)
     w_near = jnp.zeros((E, N), F32)
     t_near = jnp.zeros((E, N), F32)
@@ -723,78 +794,85 @@
     kz_near = jnp.where(up, lane32, E - 1 - lane32)
     delta_z = w_near - s_z
     alpha_z = [corners(near_r[2][at : at + 1])[0] for at in (3, 2)]
-    planes, outer = [], []
-    for which, at, kz, rows_ab, rows_h, wplane in (
-        (0, 3, kz_own, own_ab, own_h, delta_z),
-        (1, 2, kz_near, near_ab, near_h, -delta_z),
+    mark = jnp.concatenate(
+        [
+            jnp.where((sub8 == grp) & (lane32 == 0), 1.0, 0.0),
+            jnp.where((sub8 == grp) & (lane32 == E - 1), 1.0, 0.0),
+        ],
+        1,
+    )
+    weights, cols = [], []
+    for which, at, kz, rows_h, wplane in (
+        (0, 3, kz_own, own_h, delta_z),
+        (1, 2, kz_near, near_h, -delta_z),
     ):
-        weights = jnp.where(sub8 == grp, column(near_r[2][at : at + 1], kz), 0.0)
-        ca = dot(weights, rows_ab)
-        ch = dot(weights, rows_h)
+        weights.append(jnp.where(sub8 == grp, column(near_r[2][at : at + 1], kz), 0.0))
+        marked = dot_first(dot(weights[which], rows_h), mark)
+        pl_ref[which] = marked[0:E, 0:N] + marked[E : 2 * E, N : 2 * N] + alpha_z[which] * wplane
+        r1 = near_r[1][at : at + 1]
+        cols.append(
+            jnp.concatenate(
+                [
+                    jnp.where(sub8 == grp, column(r1, lane32), 0.0),
+                    jnp.where(sub8 == grp, column(r1, E - 1 - lane32), 0.0),
+                ],
+                1,
+            )
+        )
+        blocks_1[which] = packed_weights(inverse_blocks(r1))
+    blocks_1[2] = packed_weights(inverse_blocks(own[2]))
+
+    def on_face(plane, j):
+        first = roll(plane, N - j)
+        last = roll(plane, (N + E - 1 - j) & (N - 1))
+        return jnp.where(face_lane, jnp.where(up, last, first), 0.0)
+
+    pl_ref[2] = halo[0:E]
+    pl_ref[3] = halo[E : 2 * E]
+    pl_ref[4] = delta_z
+    v0, w0 = column(own[0], row32), column(own[0], E - 1 - row32)
+
+    brick_wait(send2b, land2b, 4, rs2b, own_sem.at[4])
+    own_ab, near_ab = gathered(land2b, 0), gathered(land2b, 1)
+    ab = jnp.transpose(own_ab)
+    outer = []
+    for which, rows_ab in ((0, own_ab), (1, near_ab)):
+        ca = dot(weights[which], rows_ab)
         first_row = jnp.zeros((1, N), F32)
         last_row = jnp.zeros((1, N), F32)
         for q in range(4):
             first_row = jnp.where(grp == q, roll(ca[q : q + 1], E * q), first_row)
             last_row = jnp.where(grp == q, roll(ca[q : q + 1], E * q - E), last_row)
-        mark = jnp.concatenate(
-            [
-                jnp.where((sub8 == grp) & (lane32 == 0), 1.0, 0.0),
-                jnp.where((sub8 == grp) & (lane32 == E - 1), 1.0, 0.0),
-            ],
-            1,
-        )
-        marked = dot_first(ch, mark)
-        plane = marked[0:E, 0:N] + marked[E : 2 * E, N : 2 * N] + alpha_z[which] * wplane
-        plane = plane + jnp.where(row32 == 0, first_row, 0.0)
-        plane = plane + jnp.where(row32 == E - 1, last_row, 0.0)
-        pl_ref[which] = plane
-        cols = jnp.concatenate(
-            [
-                jnp.where(sub8 == grp, column(near_r[1][at : at + 1], lane32), 0.0),
-                jnp.where(sub8 == grp, column(near_r[1][at : at + 1], E - 1 - lane32), 0.0),
-            ],
-            1,
-        )
-        sides = dot_first(ca, cols)
+        pl_ref[which, 0:1, :] = pl_ref[which, 0:1, :] + first_row
+        pl_ref[which, E - 1 : E, :] = pl_ref[which, E - 1 : E, :] + last_row
+        sides = dot_first(ca, cols[which])
         outer.append(sides[64:96, 0:N] + sides[96:128, N : 2 * N])
-
-    halo_low, halo_up = halo[0:E], halo[E : 2 * E]
-    f_ref[0:E, :] = f_ref[0:E, :] + halo_low
-    f_ref[(E - 1) * E : E * E, :] = f_ref[(E - 1) * E : E * E, :] + halo_up
-    at = pl.ds(0, E, stride=E)
-    f_ref[at, :] = f_ref[at, :] + ab[0:E]
-    at = pl.ds(E - 1, E, stride=E)
-    f_ref[at, :] = f_ref[at, :] + ab[E : 2 * E]
-
-    def on_face(plane, j):
-        first = roll(plane, N - j)
-        last = roll(plane, (N + E - 1 - j) & (N - 1))
-        return jnp.where(face_lane, jnp.where(up, last, first), 0.0)
-
-    def z_halo(t, carry):
-        for m in range(4):
-            j = t * 4 + m
-            at = pl.ds(pl.multiple_of(j * E, E), E)
-            f_ref[at, :] = f_ref[at, :] + on_face(delta_z, j)
-        return carry
-
-    lax.fori_loop(0, E // 4, z_halo, 0)
-
-    def last_rows(i):
-        x = jnp.where(sub8 == 3, pl_ref[0, pl.ds(i, 1), :], 0.0)
-        return jnp.where(sub8 == 2, pl_ref[1, pl.ds(i, 1), :], x)
-
-    solve_i(last_rows)
+    h = jnp.zeros((8, N), F32)
+    for i in range(E):
+        x = jnp.where(sub8 == 2, pl_ref[1, i : i + 1, :], pl_ref[0, i : i + 1, :])
+        for at, p in ((4, 2), (5, 3), (6, 4)):
+            x = jnp.where(sub8 == at, pl_ref[p, i : i + 1, :], x)
+        h = ecm[i] * x + ece[i] * h
+        e_ref[i] = h
+    for i in range(E - 2, -1, -1):
+        h = e_ref[i] + ece[i] * h
+        e_ref[i] = h
+    z_part = e_ref[:, 6, :]
     ends_z = []
     for which, at in ((0, 3), (1, 2)):
-        blocks = inverse_blocks(near_r[1][at : at + 1])
-        ends_z.append(dot(e_ref[:, at, :], blocks) + outer[which])
+        ends_z.append(packed_dot(e_ref[:, at, :], blocks_1[which]) + outer[which])
     sigma = ends_z[0] + t_own
     tau = ends_z[1] + t_near
     c_plane = -gz * (sigma - tau) / (1.0 + gz * (alpha_z[0] + alpha_z[1]))
 
-    solve_j(ab[64:96], ab[96:128])
-    zblocks = packed_weights(inverse_blocks(own[2]))
+    ab_ref[...] = ab
+
+    def answer(j):
+        at_lower, at_upper = ab_ref[pl.ds(j, 1), :], ab_ref[pl.ds(E + j, 1), :]
+        return v0 * at_lower + w0 * at_upper + on_face(z_part, j)
+
+    solve_j(answer, ab[64:96] + e_ref[:, 4, :], ab[96:128] + e_ref[:, 5, :])
+    zblocks = blocks_1[2]
 
     def finish(t, carry):
         d2 = []
@@ -802,7 +880,8 @@
             at = pl.ds(pl.multiple_of((t * 8 + m) * E, E), E)
             d2.append(g_ref[at, :] + on_face(c_plane, t * 8 + m))
         d3 = packed_dot(jnp.concatenate(d2, 0), zblocks)
-        d3 = d3 + u_ref[pl.ds(pl.multiple_of(t * 8 * E, 8 * E), 8 * E), :]
+        at = pl.ds(pl.multiple_of(t * 8 * E, 8 * E), 8 * E)
+        d3 = d3 + u_ref[at, :]
         for half in range(2):
             outs = swap_blocks(
                 [d3[(half * 4 + m) * E : (half * 4 + m + 1) * E] for m in range(4)], grp
@@ -817,24 +896,26 @@
 
     for at in range(2):
         gather_all(at).wait_send()
-
-    def left1(count):
-        part = send1.at[pl.ds(0, 8 * count)]
+    to_owners_wait(send1b, 6, ss1b)
+
+    def left_c(count):
+        part = send1c.at[pl.ds(0, 4 * count)]
         pltpu.make_async_remote_copy(
-            part, part, ss1, rs1, device_id=(me,), device_id_type=MESH
+            part, part, ss1c, ss1c, device_id=(me,), device_id_type=MESH
         ).wait_send()
+
+    @pl.when(at_face)
+    def _():
+        left_c(3)
+
+    @pl.when(jnp.logical_not(at_face))
+    def _():
+        left_c(4)
 
     @pl.when(owner)
     def _():
-        left1(OWNERS - 1)
-        part = send2.at[pl.ds(0, 8 * (N - 1))]
-        pltpu.make_async_remote_copy(
-            part, part, ss2, rs2, device_id=(me,), device_id_type=MESH
-        ).wait_send()
-
-    @pl.when(jnp.logical_not(owner))
-    def _():
-        left1(OWNERS)
+        to_bricks_wait(send2a, 4, ss2a)
+        to_bricks_wait(send2b, 4, ss2b)
 
 
 def body(calcium, buffer, fraction, rates, inverses, neighbors, ranks):
@@ -855,22 +936,28 @@
             pltpu.VMEM((N, 1, N), F32),
             pltpu.VMEM((8 * OWNERS, N), F32),
             pltpu.VMEM((8 * N, N), F32),
-            pltpu.VMEM((8 * N, N), F32),
-            pltpu.VMEM((8 * OWNERS, N), F32),
+            pltpu.VMEM((16, N), F32),
+            pltpu.VMEM((4 * N, N), F32),
+            pltpu.VMEM((4 * N, N), F32),
+            pltpu.VMEM((4 * OWNERS, N), F32),
+            pltpu.VMEM((4 * N, N), F32),
+            pltpu.VMEM((4 * OWNERS, N), F32),
+            pltpu.VMEM((3, 256, 256), BF16),
             pltpu.VMEM((3, E, N), F32),
             pltpu.VMEM((3, E, N), F32),
             pltpu.VMEM((E, 8, N), F32),
             pltpu.VMEM((E, 8, N), F32),
             pltpu.VMEM((E, 8, N), F32),
-            pltpu.VMEM((3, E, N), F32),
+            pltpu.VMEM((5, E, N), F32),
+            pltpu.VMEM((N, N), F32),
             pltpu.VMEM((4, 256, N), BF16),
             pltpu.VMEM((4, N, 256), BF16),
             pltpu.VMEM((19, 256, N), F32),
-            pltpu.VMEM((11, 256, N), F32),
+            pltpu.VMEM((12, 256, N), F32),
         ]
         + [pltpu.SemaphoreType.DMA((2,))] * 2
-        + [pltpu.SemaphoreType.DMA] * 4
-        + [pltpu.SemaphoreType.DMA((2,))],
+        + [pltpu.SemaphoreType.DMA] * 8
+        + [pltpu.SemaphoreType.DMA((5,))],
         compiler_params=pltpu.CompilerParams(
             collective_id=0, has_side_effects=True, vmem_limit_bytes=60 * 1024 * 1024
         ),

time: 45.4 us -> 44.2 us (0.974)
  Pallas kernels: 42.2 us -> 41 us
    pallas_call x1, Pallas kernels: 42.2 us -> 41 us  [body(): pl.pallas_call(step_kernel, out_shape=(shape, shape), in_specs=[smem, sme...]
where the time goes in v5:
time: 44.2 us; the launch traced here: 44 us
  Pallas kernels  41 us (93%)
  local copies, waits for them, and re-layouts  2.42 us (5%)
  between operations  0.65 us (1%)
    pallas_call x1, Pallas kernels, body(): pl.pallas_call(step_kernel, out_shape=(shape, shape), in_specs=[smem, sme...  41 us
    unnamed x4, local copies, waits for them, and re-layouts  2.42 us

profile of v5, /device:TPU:1, one launch (start us, length us, event | category | flops | bytes accessed | tf_op | source)
XLA Modules:
  0.0 44.0 jit_solution(13739941245852032265)
XLA Ops:
  0.6 41.0 %shard_map.77 = (f32[2,32,1024]{2,1,0:T(8,128)}, f32[2,32,1024]{2,1,0:T(8,128)}) custom-call(f32[2,2,3]{2,1,0:T(2,128)} %bitcast.1, s32[3,2,256]{2,1,0:T(2,128)} %nbv.1, s32[3,2,256]{2,1,0:T(2,128)} %nbv.1, s32[3,256]{1,0:T(4,128)} %rkv.1, f32[2,32,1024]{2,1,0:T(8,128)} %cal.1, f32[2,32,1024]{2,1,0:T(8,128)} %buf.1, f32[2,32,1024]{2,1,0:T(8,128)} %frac.1), custom_call_target="tpu_custom_call" | custom-call | tf_op jit(solution)/shard_map/pallas_call | solution.py:926
  41.6 0.0 copy-start
  41.6 1.7 %copy.10 = f32[2,32,1024]{2,1,0:T(8,128)} copy(f32[2,32,1024]{2,1,0:T(8,128)} %get-tuple-element.4) | data formatting | bytes 524288
  43.3 0.0 copy-done
  43.3 0.7 %copy.11 = f32[2,32,1024]{2,1,0:T(8,128)} copy(f32[2,32,1024]{2,1,0:T(8,128)S(1)} %copy-done) | data formatting | bytes 524288
Async XLA Ops:
  41.6 1.7 %copy-start = (f32[2,32,1024]{2,1,0:T(8,128)S(1)}, f32[2,32,1024]{2,1,0:T(8,128)}, u32[]{:S(2)}) copy-start(f32[2,32,1024]{2,1,0:T(8,128)} %get-tuple-element.5) | copy-start | bytes 786436

commit v6 on v5

--- a/solution.py
+++ b/solution.py
@@ -264,9 +264,6 @@
         return jnp.where(lane32 == j, jnp.where(up, last, first), plane)
 
     wz = lax.fori_loop(0, E, face, jnp.zeros((E, N), F32))
-
-    gather_all(0).wait_recv()
-    gather_start(1)
 
     cu2 = jnp.where(lane32 < E - 1, 2.0 * own[2], 0.0)
     cd2 = jnp.where(lane32 > 0, 2.0 * own[2], 0.0)
@@ -296,6 +293,9 @@
         return prev
 
     lax.fori_loop(0, E // 4, right_side, jnp.zeros((E, N), F32))
+
+    gather_all(0).wait_recv()
+    gather_start(1)
 
     def solve_i(load_plane_row):
         def forward(t, carry):

time: 44.2 us -> 43.3 us (0.980)
  Pallas kernels: 41 us -> 40.1 us
    pallas_call x1, Pallas kernels: 41 us -> 40.1 us  [body(): pl.pallas_call(step_kernel, out_shape=(shape, shape), in_specs=[smem, sme...]
where the time goes in v6:
time: 43.3 us; the launch traced here: 43.2 us
  Pallas kernels  40.1 us (93%)
  local copies, waits for them, and re-layouts  2.42 us (6%)
  between operations  0.65 us (2%)
    pallas_call x1, Pallas kernels, body(): pl.pallas_call(step_kernel, out_shape=(shape, shape), in_specs=[smem, sme...  40.1 us
    unnamed x4, local copies, waits for them, and re-layouts  2.42 us

profile of v6, /device:TPU:1, one launch (start us, length us, event | category | flops | bytes accessed | tf_op | source)
XLA Modules:
  0.0 43.2 jit_solution(10145839815876268405)
XLA Ops:
  0.6 40.1 %shard_map.77 = (f32[2,32,1024]{2,1,0:T(8,128)}, f32[2,32,1024]{2,1,0:T(8,128)}) custom-call(f32[2,2,3]{2,1,0:T(2,128)} %bitcast.1, s32[3,2,256]{2,1,0:T(2,128)} %nbv.1, s32[3,2,256]{2,1,0:T(2,128)} %nbv.1, s32[3,256]{1,0:T(4,128)} %rkv.1, f32[2,32,1024]{2,1,0:T(8,128)} %cal.1, f32[2,32,1024]{2,1,0:T(8,128)} %buf.1, f32[2,32,1024]{2,1,0:T(8,128)} %frac.1), custom_call_target="tpu_custom_call" | custom-call | tf_op jit(solution)/shard_map/pallas_call | solution.py:926
  40.7 0.0 copy-start
  40.8 1.7 %copy.10 = f32[2,32,1024]{2,1,0:T(8,128)} copy(f32[2,32,1024]{2,1,0:T(8,128)} %get-tuple-element.4) | data formatting | bytes 524288
  42.5 0.0 copy-done
  42.5 0.7 %copy.11 = f32[2,32,1024]{2,1,0:T(8,128)} copy(f32[2,32,1024]{2,1,0:T(8,128)S(1)} %copy-done) | data formatting | bytes 524288
Async XLA Ops:
  40.7 1.7 %copy-start = (f32[2,32,1024]{2,1,0:T(8,128)S(1)}, f32[2,32,1024]{2,1,0:T(8,128)}, u32[]{:S(2)}) copy-start(f32[2,32,1024]{2,1,0:T(8,128)} %get-tuple-element.5) | copy-start | bytes 786436

commit v7 on v6

--- a/solution.py
+++ b/solution.py
@@ -235,240 +235,7 @@
         co[1] = e
         co[2] = jnp.where(row32 == E - 1, 0.0, e)
 
-    pl.semaphore_wait(barrier, len(greeted))
-
-    def rates_block(unit):
-        return rt.at[pl.ds(me & (N - unit), unit)]
-
-    def gather_start(at):
-        unit, group = stages[at]
-        for to in group:
-            pltpu.make_async_remote_copy(
-                rates_block(unit), rates_block(unit), ss0.at[at], rs0.at[at],
-                device_id=(to,), device_id_type=MESH,
-            ).start()
-
-    def gather_all(at):
-        unit, group = stages[at]
-        part = rt.at[pl.ds(0, unit * len(group))]
-        return pltpu.make_async_remote_copy(
-            part, part, ss0.at[at], rs0.at[at], device_id=(me,), device_id_type=MESH
-        )
-
-    gather_start(0)
-
-    def face(j, plane):
-        u = u_ref[pl.ds(pl.multiple_of(j * E, E), E), :]
-        first = roll(u, j)
-        last = roll(u, j + (N - E + 1))
-        return jnp.where(lane32 == j, jnp.where(up, last, first), plane)
-
-    wz = lax.fori_loop(0, E, face, jnp.zeros((E, N), F32))
-
-    cu2 = jnp.where(lane32 < E - 1, 2.0 * own[2], 0.0)
-    cd2 = jnp.where(lane32 > 0, 2.0 * own[2], 0.0)
-    dg2 = cu2 + cd2
-    r1x2 = 2.0 * own[1]
-
-    def right_side(t, prev):
-        us = []
-        for m in range(5):
-            j = jnp.minimum(t * 4 + m, E - 1)
-            us.append(u_ref[pl.ds(pl.multiple_of(j * E, E), E), :])
-        for m in range(4):
-            j = t * 4 + m
-            at = pl.ds(pl.multiple_of(j * E, E), E)
-            u = us[m]
-            low = jnp.where(j == 0, 0.0, r1x2)
-            high = jnp.where(j == E - 1, 0.0, r1x2)
-            f_ref[at, :] = (
-                f_ref[at, :]
-                + cu2 * roll(u, -1)
-                + cd2 * roll(u, 1)
-                + low * prev
-                + high * us[m + 1]
-                - (dg2 + low + high) * u
-            )
-            prev = u
-        return prev
-
-    lax.fori_loop(0, E // 4, right_side, jnp.zeros((E, N), F32))
-
-    gather_all(0).wait_recv()
-    gather_start(1)
-
-    def solve_i(load_plane_row):
-        def forward(t, carry):
-            g, h = carry
-            for m in range(4):
-                i = t * 4 + m
-                at = pl.ds(i, E, stride=E)
-                g = co0[0, pl.ds(i, 1), :] * f_ref[at, :] + co0[1, pl.ds(i, 1), :] * g
-                t_ref[at, :] = g
-                if load_plane_row is not None:
-                    h = ecm[i] * load_plane_row(i) + ece[i] * h
-                    e_ref[i] = h
-            return g, h
-
-        lax.fori_loop(0, E // 4, forward, (jnp.zeros((E, N), F32), jnp.zeros((8, N), F32)))
-
-        def backward(t, carry):
-            x, h = carry
-            for m in range(4):
-                i = E - 1 - t * 4 - m
-                at = pl.ds(i, E, stride=E)
-                x = t_ref[at, :] + co0[2, pl.ds(i, 1), :] * x
-                t_ref[at, :] = x
-                if load_plane_row is not None:
-                    h = e_ref[i] + jnp.where(i == E - 1, 0.0, ece[i]) * h
-                    e_ref[i] = h
-            return x, h
-
-        lax.fori_loop(0, E // 4, backward, (jnp.zeros((E, N), F32), jnp.zeros((8, N), F32)))
-
-    def solve_j(extra, extra_first, extra_last):
-        def forward(t, g):
-            for m in range(4):
-                j = t * 4 + m
-                at = pl.ds(pl.multiple_of(j * E, E), E)
-                d = t_ref[at, :] - 2.0 * u_ref[at, :]
-                if extra is not None:
-                    d = d + extra(j)
-                if extra_first is not None and m == 0:
-                    d = d + jnp.where(j == 0, extra_first, 0.0)
-                if extra_last is not None and m == 3:
-                    d = d + jnp.where(j == E - 1, extra_last, 0.0)
-                g = co1[0, pl.ds(j, 1), :] * d + co1[1, pl.ds(j, 1), :] * g
-                g_ref[at, :] = g
-            return g
-
-        lax.fori_loop(0, E // 4, forward, jnp.zeros((E, N), F32))
-
-        def backward(t, x):
-            for m in range(4):
-                j = E - 1 - t * 4 - m
-                at = pl.ds(pl.multiple_of(j * E, E), E)
-                x = g_ref[at, :] + co1[2, pl.ds(j, 1), :] * x
-                g_ref[at, :] = x
-            return x
-
-        lax.fori_loop(0, E // 4, backward, jnp.zeros((E, N), F32))
-
-    solve_i(None)
-    solve_j(None, None, None)
-
-    rowN, colN = iota((N, N), 0), iota((N, N), 1)
-    kin = rowN & 31
-    weight = column(own[2], jnp.where(up, E - 1 - kin, kin))
-    weight = packed_weights(jnp.where((rowN >> 5) == (colN >> 5), weight, 0.0))
-
-    def face_mean(t, plane):
-        y = packed_dot(g_ref[pl.ds(pl.multiple_of(t * 8 * E, 8 * E), 8 * E), :], weight)
-        for m in range(8):
-            plane = jnp.where(lane32 == t * 8 + m, y[m * E : (m + 1) * E], plane)
-        return plane
-
-    t_own = lax.fori_loop(0, 4, face_mean, jnp.zeros((E, N), F32))
-
-    rows_a = jnp.transpose(
-        jnp.concatenate(
-            [
-                t_ref[pl.ds(0, E, stride=E), :],
-                t_ref[pl.ds(E - 1, E, stride=E), :],
-                g_ref[0:E, :],
-                g_ref[(E - 1) * E : E * E, :],
-            ],
-            0,
-        )
-    )
-    for q in range(4):
-        send1b[pl.ds(8 * (q % 2) + 3 * (q // 2), E, stride=16), :] = rows_a[q * E : (q + 1) * E]
-    mine = me >> 1
-
-    def block(ref, index, rows):
-        pitch = 8 if rows == 6 else rows
-        return ref.at[pl.ds(pl.multiple_of(index * pitch, pitch), rows)]
-
-    def to_owners(src, dst, rows, send_sem, recv_sem, local_sem):
-        def send(step, carry):
-            o = (mine + step) & (OWNERS - 1)
-            pltpu.make_async_remote_copy(
-                block(src, o, rows), block(dst, me, rows), send_sem, recv_sem,
-                device_id=(2 * o,), device_id_type=MESH,
-            ).start()
-            return carry
-
-        lax.fori_loop(1, OWNERS, send, 0)
-
-        @pl.when(jnp.logical_not(owner))
-        def _():
-            pltpu.make_async_remote_copy(
-                block(src, mine, rows), block(dst, me, rows), send_sem, recv_sem,
-                device_id=(2 * mine,), device_id_type=MESH,
-            ).start()
-
-        @pl.when(owner)
-        def _():
-            pltpu.make_async_copy(block(src, mine, rows), block(dst, me, rows), local_sem).start()
-
-    def to_owners_wait(src, rows, send_sem):
-        def left(count):
-            part = src.at[pl.ds(0, count * rows)]
-            pltpu.make_async_remote_copy(
-                part, part, send_sem, send_sem, device_id=(me,), device_id_type=MESH
-            ).wait_send()
-
-        @pl.when(owner)
-        def _():
-            left(OWNERS - 1)
-
-        @pl.when(jnp.logical_not(owner))
-        def _():
-            left(OWNERS)
-
-    def owner_wait(src, dst, rows, recv_sem, local_sem):
-        pltpu.make_async_copy(block(src, mine, rows), block(dst, me, rows), local_sem).wait()
-        part = dst.at[pl.ds(0, rows * (N - 1))]
-        pltpu.make_async_remote_copy(
-            part, part, recv_sem, recv_sem, device_id=(me,), device_id_type=MESH
-        ).wait_recv()
-
-    def to_bricks(src, dst, rows, send_sem, recv_sem, local_sem):
-        def send(step, carry):
-            to = (me + step) & (N - 1)
-            pltpu.make_async_remote_copy(
-                block(src, to, rows), block(dst, mine, rows), send_sem, recv_sem,
-                device_id=(to,), device_id_type=MESH,
-            ).start()
-            return carry
-
-        lax.fori_loop(1, N, send, 0)
-        pltpu.make_async_copy(block(src, me, rows), block(dst, mine, rows), local_sem).start()
-
-    def to_bricks_wait(src, rows, send_sem):
-        part = src.at[pl.ds(0, rows * (N - 1))]
-        pltpu.make_async_remote_copy(
-            part, part, send_sem, send_sem, device_id=(me,), device_id_type=MESH
-        ).wait_send()
-
-    def brick_wait(src, dst, rows, recv_sem, local_sem):
-        def arrived(count):
-            part = dst.at[pl.ds(0, count * rows)]
-            pltpu.make_async_remote_copy(
-                part, part, recv_sem, recv_sem, device_id=(me,), device_id_type=MESH
-            ).wait_recv()
-
-        @pl.when(owner)
-        def _():
-            pltpu.make_async_copy(block(src, me, rows), block(dst, mine, rows), local_sem).wait()
-            arrived(OWNERS - 1)
-
-        @pl.when(jnp.logical_not(owner))
-        def _():
-            arrived(OWNERS)
-
     owner = (me & 1) == 0
-
     @pl.when(owner)
     def _():
         s2, l2 = iota((256, 256), 0), iota((256, 256), 1)
@@ -506,6 +273,239 @@
             posz_b = total(jnp.where(lf == z_b, pos + 1.0, 0.0), 1) - 1.0
             permt[b] = one_hot(lf == pos_b)
             permt[2 + b] = one_hot(lf == posz_b)
+
+    pl.semaphore_wait(barrier, len(greeted))
+
+    def rates_block(unit):
+        return rt.at[pl.ds(me & (N - unit), unit)]
+
+    def gather_start(at):
+        unit, group = stages[at]
+        for to in group:
+            pltpu.make_async_remote_copy(
+                rates_block(unit), rates_block(unit), ss0.at[at], rs0.at[at],
+                device_id=(to,), device_id_type=MESH,
+            ).start()
+
+    def gather_all(at):
+        unit, group = stages[at]
+        part = rt.at[pl.ds(0, unit * len(group))]
+        return pltpu.make_async_remote_copy(
+            part, part, ss0.at[at], rs0.at[at], device_id=(me,), device_id_type=MESH
+        )
+
+    gather_start(0)
+
+    def face(j, plane):
+        u = u_ref[pl.ds(pl.multiple_of(j * E, E), E), :]
+        first = roll(u, j)
+        last = roll(u, j + (N - E + 1))
+        return jnp.where(lane32 == j, jnp.where(up, last, first), plane)
+
+    wz = lax.fori_loop(0, E, face, jnp.zeros((E, N), F32))
+
+    cu2 = jnp.where(lane32 < E - 1, 2.0 * own[2], 0.0)
+    cd2 = jnp.where(lane32 > 0, 2.0 * own[2], 0.0)
+    dg2 = cu2 + cd2
+    r1x2 = 2.0 * own[1]
+
+    def right_side(t, prev):
+        us = []
+        for m in range(5):
+            j = jnp.minimum(t * 4 + m, E - 1)
+            us.append(u_ref[pl.ds(pl.multiple_of(j * E, E), E), :])
+        for m in range(4):
+            j = t * 4 + m
+            at = pl.ds(pl.multiple_of(j * E, E), E)
+            u = us[m]
+            low = jnp.where(j == 0, 0.0, r1x2)
+            high = jnp.where(j == E - 1, 0.0, r1x2)
+            f_ref[at, :] = (
+                f_ref[at, :]
+                + cu2 * roll(u, -1)
+                + cd2 * roll(u, 1)
+                + low * prev
+                + high * us[m + 1]
+                - (dg2 + low + high) * u
+            )
+            prev = u
+        return prev
+
+    lax.fori_loop(0, E // 4, right_side, jnp.zeros((E, N), F32))
+
+    gather_all(0).wait_recv()
+    gather_start(1)
+
+    def solve_i(load_plane_row):
+        def forward(t, carry):
+            g, h = carry
+            for m in range(4):
+                i = t * 4 + m
+                at = pl.ds(i, E, stride=E)
+                g = co0[0, pl.ds(i, 1), :] * f_ref[at, :] + co0[1, pl.ds(i, 1), :] * g
+                t_ref[at, :] = g
+                if load_plane_row is not None:
+                    h = ecm[i] * load_plane_row(i) + ece[i] * h
+                    e_ref[i] = h
+            return g, h
+
+        lax.fori_loop(0, E // 4, forward, (jnp.zeros((E, N), F32), jnp.zeros((8, N), F32)))
+
+        def backward(t, carry):
+            x, h = carry
+            for m in range(4):
+                i = E - 1 - t * 4 - m
+                at = pl.ds(i, E, stride=E)
+                x = t_ref[at, :] + co0[2, pl.ds(i, 1), :] * x
+                t_ref[at, :] = x
+                if load_plane_row is not None:
+                    h = e_ref[i] + jnp.where(i == E - 1, 0.0, ece[i]) * h
+                    e_ref[i] = h
+            return x, h
+
+        lax.fori_loop(0, E // 4, backward, (jnp.zeros((E, N), F32), jnp.zeros((8, N), F32)))
+
+    def solve_j(extra, extra_first, extra_last):
+        def forward(t, g):
+            for m in range(4):
+                j = t * 4 + m
+                at = pl.ds(pl.multiple_of(j * E, E), E)
+                d = t_ref[at, :] - 2.0 * u_ref[at, :]
+                if extra is not None:
+                    d = d + extra(j)
+                if extra_first is not None and m == 0:
+                    d = d + jnp.where(j == 0, extra_first, 0.0)
+                if extra_last is not None and m == 3:
+                    d = d + jnp.where(j == E - 1, extra_last, 0.0)
+                g = co1[0, pl.ds(j, 1), :] * d + co1[1, pl.ds(j, 1), :] * g
+                g_ref[at, :] = g
+            return g
+
+        lax.fori_loop(0, E // 4, forward, jnp.zeros((E, N), F32))
+
+        def backward(t, x):
+            for m in range(4):
+                j = E - 1 - t * 4 - m
+                at = pl.ds(pl.multiple_of(j * E, E), E)
+                x = g_ref[at, :] + co1[2, pl.ds(j, 1), :] * x
+                g_ref[at, :] = x
+            return x
+
+        lax.fori_loop(0, E // 4, backward, jnp.zeros((E, N), F32))
+
+    solve_i(None)
+    solve_j(None, None, None)
+
+    rowN, colN = iota((N, N), 0), iota((N, N), 1)
+    kin = rowN & 31
+    weight = column(own[2], jnp.where(up, E - 1 - kin, kin))
+    weight = packed_weights(jnp.where((rowN >> 5) == (colN >> 5), weight, 0.0))
+
+    def face_mean(t, plane):
+        y = packed_dot(g_ref[pl.ds(pl.multiple_of(t * 8 * E, 8 * E), 8 * E), :], weight)
+        for m in range(8):
+            plane = jnp.where(lane32 == t * 8 + m, y[m * E : (m + 1) * E], plane)
+        return plane
+
+    t_own = lax.fori_loop(0, 4, face_mean, jnp.zeros((E, N), F32))
+
+    rows_a = jnp.transpose(
+        jnp.concatenate(
+            [
+                t_ref[pl.ds(0, E, stride=E), :],
+                t_ref[pl.ds(E - 1, E, stride=E), :],
+                g_ref[0:E, :],
+                g_ref[(E - 1) * E : E * E, :],
+            ],
+            0,
+        )
+    )
+    for q in range(4):
+        send1b[pl.ds(8 * (q % 2) + 3 * (q // 2), E, stride=16), :] = rows_a[q * E : (q + 1) * E]
+    mine = me >> 1
+
+    def block(ref, index, rows):
+        pitch = 8 if rows == 6 else rows
+        return ref.at[pl.ds(pl.multiple_of(index * pitch, pitch), rows)]
+
+    def to_owners(src, dst, rows, send_sem, recv_sem, local_sem):
+        def send(step, carry):
+            o = (mine + step) & (OWNERS - 1)
+            pltpu.make_async_remote_copy(
+                block(src, o, rows), block(dst, me, rows), send_sem, recv_sem,
+                device_id=(2 * o,), device_id_type=MESH,
+            ).start()
+            return carry
+
+        lax.fori_loop(1, OWNERS, send, 0)
+
+        @pl.when(jnp.logical_not(owner))
+        def _():
+            pltpu.make_async_remote_copy(
+                block(src, mine, rows), block(dst, me, rows), send_sem, recv_sem,
+                device_id=(2 * mine,), device_id_type=MESH,
+            ).start()
+
+        @pl.when(owner)
+        def _():
+            pltpu.make_async_copy(block(src, mine, rows), block(dst, me, rows), local_sem).start()
+
+    def to_owners_wait(src, rows, send_sem):
+        def left(count):
+            part = src.at[pl.ds(0, count * rows)]
+            pltpu.make_async_remote_copy(
+                part, part, send_sem, send_sem, device_id=(me,), device_id_type=MESH
+            ).wait_send()
+
+        @pl.when(owner)
+        def _():
+            left(OWNERS - 1)
+
+        @pl.when(jnp.logical_not(owner))
+        def _():
+            left(OWNERS)
+
+    def owner_wait(src, dst, rows, recv_sem, local_sem):
+        pltpu.make_async_copy(block(src, mine, rows), block(dst, me, rows), local_sem).wait()
+        part = dst.at[pl.ds(0, rows * (N - 1))]
+        pltpu.make_async_remote_copy(
+            part, part, recv_sem, recv_sem, device_id=(me,), device_id_type=MESH
+        ).wait_recv()
+
+    def to_bricks(src, dst, rows, send_sem, recv_sem, local_sem):
+        def send(step, carry):
+            to = (me + step) & (N - 1)
+            pltpu.make_async_remote_copy(
+                block(src, to, rows), block(dst, mine, rows), send_sem, recv_sem,
+                device_id=(to,), device_id_type=MESH,
+            ).start()
+            return carry
+
+        lax.fori_loop(1, N, send, 0)
+        pltpu.make_async_copy(block(src, me, rows), block(dst, mine, rows), local_sem).start()
+
+    def to_bricks_wait(src, rows, send_sem):
+        part = src.at[pl.ds(0, rows * (N - 1))]
+        pltpu.make_async_remote_copy(
+            part, part, send_sem, send_sem, device_id=(me,), device_id_type=MESH
+        ).wait_send()
+
+    def brick_wait(src, dst, rows, recv_sem, local_sem):
+        def arrived(count):
+            part = dst.at[pl.ds(0, count * rows)]
+            pltpu.make_async_remote_copy(
+                part, part, recv_sem, recv_sem, device_id=(me,), device_id_type=MESH
+            ).wait_recv()
+
+        @pl.when(owner)
+        def _():
+            pltpu.make_async_copy(block(src, me, rows), block(dst, mine, rows), local_sem).wait()
+            arrived(OWNERS - 1)
+
+        @pl.when(jnp.logical_not(owner))
+        def _():
+            arrived(OWNERS)
+
 
     gather_all(1).wait_recv()
 

time: 43.3 us -> 43.9 us (1.014)
  Pallas kernels: 40.1 us -> 40.7 us
    pallas_call x1, Pallas kernels: 40.1 us -> 40.7 us  [body(): pl.pallas_call(step_kernel, out_shape=(shape, shape), in_specs=[smem, sme...]
where the time goes in v7:
time: 43.9 us; the launch traced here: 43.8 us
  Pallas kernels  40.7 us (93%)
  local copies, waits for them, and re-layouts  2.42 us (6%)
  between operations  0.65 us (1%)
    pallas_call x1, Pallas kernels, body(): pl.pallas_call(step_kernel, out_shape=(shape, shape), in_specs=[smem, sme...  40.7 us
    unnamed x4, local copies, waits for them, and re-layouts  2.42 us

profile of v7, /device:TPU:1, one launch (start us, length us, event | category | flops | bytes accessed | tf_op | source)
XLA Modules:
  0.0 43.8 jit_solution(2364257351380787915)
XLA Ops:
  0.6 40.7 %shard_map.77 = (f32[2,32,1024]{2,1,0:T(8,128)}, f32[2,32,1024]{2,1,0:T(8,128)}) custom-call(f32[2,2,3]{2,1,0:T(2,128)} %bitcast.1, s32[3,2,256]{2,1,0:T(2,128)} %nbv.1, s32[3,2,256]{2,1,0:T(2,128)} %nbv.1, s32[3,256]{1,0:T(4,128)} %rkv.1, f32[2,32,1024]{2,1,0:T(8,128)} %cal.1, f32[2,32,1024]{2,1,0:T(8,128)} %buf.1, f32[2,32,1024]{2,1,0:T(8,128)} %frac.1), custom_call_target="tpu_custom_call" | custom-call | tf_op jit(solution)/shard_map/pallas_call | solution.py:926
  41.3 0.0 copy-start
  41.4 1.7 %copy.10 = f32[2,32,1024]{2,1,0:T(8,128)} copy(f32[2,32,1024]{2,1,0:T(8,128)} %get-tuple-element.4) | data formatting | bytes 524288
  43.1 0.0 copy-done
  43.1 0.7 %copy.11 = f32[2,32,1024]{2,1,0:T(8,128)} copy(f32[2,32,1024]{2,1,0:T(8,128)S(1)} %copy-done) | data formatting | bytes 524288
Async XLA Ops:
  41.3 1.7 %copy-start = (f32[2,32,1024]{2,1,0:T(8,128)S(1)}, f32[2,32,1024]{2,1,0:T(8,128)}, u32[]{:S(2)}) copy-start(f32[2,32,1024]{2,1,0:T(8,128)} %get-tuple-element.5) | copy-start | bytes 786436
